TPU v7x, 32 devices: a whole 2x2x4 slice. The times are simulated.
32 devices in a mesh: rep: 1, ctx: 32 (over z, y, x, core), fsdp: 1.
Axes of the slice: x: 2, y: 2, z: 4, core: 2. Of those that a mesh axis runs over, the one named last changes fastest.
Arguments:
- projected_queries: bfloat16 [4096, 2, 2048], P(('rep', 'ctx'), None, 'fsdp'), may hold values from -5 to 5
- projected_keys: bfloat16 [4096, 2, 256], P(('rep', 'ctx'), None, 'fsdp'), may hold values from -5 to 5
- projected_values: bfloat16 [4096, 2, 256], P(('rep', 'ctx'), None, 'fsdp'), may hold values from -6 to 6
- output_gradient: bfloat16 [4096, 2, 2048], P(('rep', 'ctx'), None, 'fsdp'), may hold values from -24 to 24
- normed_layer_input: bfloat16 [4096, 8192], P(('rep', 'ctx'), 'fsdp'), may hold values from -6 to 6
- segment: int32 [4096], P('rep'), may hold values from 0 to 2, as said below
- query_adapter_down: bfloat16 [16, 8192], P(None, 'fsdp'), may hold values from -0.0625 to 0.0625
- query_adapter_up: bfloat16 [16, 2, 2048], P(None, None, 'fsdp'), may hold values from -1.5 to 1.5
- value_adapter_down: bfloat16 [16, 8192], P(None, 'fsdp'), may hold values from -0.0625 to 0.0625
- value_adapter_up: bfloat16 [16, 2, 256], P(None, None, 'fsdp'), may hold values from -1.5 to 1.5
Outputs:
- grad_query: bfloat16 [4096, 2, 2048], P(('rep', 'ctx'), None, 'fsdp')
- grad_key: bfloat16 [4096, 2, 256], P(('rep', 'ctx'), None, 'fsdp')
- grad_value: bfloat16 [4096, 2, 256], P(('rep', 'ctx'), None, 'fsdp')
- query_down_gradient: float32 [16, 8192], P('rep', 'fsdp')
- query_up_gradient: float32 [16, 2, 2048], P('rep', None, 'fsdp')
- value_down_gradient: float32 [16, 8192], P('rep', 'fsdp')
- value_up_gradient: float32 [16, 2, 256], P('rep', None, 'fsdp')
Inputs may be any that keep to these rules, and one draw needn't show every extreme that they name: `segment`: documents are packed cyclically: ids rise by one at each of two boundaries, and a third boundary returns to id 0, whose document continues at the start of the token order; all boundaries lie at least 1024 tokens from both ends.
All inputs are finite; a program needn't handle non-finite values.
Results may differ from a plain program's by a relative error of at most 0.0079.
Values may be sent and summed in bfloat16 or wider, within the bound.
A program may use at most 64 MiB of HBM per device.

v0:
```python
import jax
import jax.numpy as jnp
from jax import lax
from jax.sharding import PartitionSpec as P

QUERY_HEADS = 32
KEY_VALUE_HEADS = 4
HEAD_SIZE = 128
GROUP = 1024


adapter_scale = 2.0


def shifted(x, axis, by):
    size = lax.axis_size(axis)
    return lax.ppermute(x, axis, [(i, (i + by) % size) for i in range(size)])


def attend(query_part, grad_part, key_rows, value_rows, allowed):
    scaling = query_part.shape[-1] ** (-0.5)
    scores = (
        jnp.einsum("tgrd,lgd->tgrl", query_part, key_rows, preferred_element_type=jnp.float32)
        * scaling
    )
    scores = jnp.where(allowed[:, None, None, :], scores, -jnp.inf)
    highest = jnp.max(scores, axis=-1, keepdims=True)
    weights = jnp.exp(scores - highest)
    weights = weights / jnp.sum(weights, axis=-1, keepdims=True)
    rounded = weights.astype(jnp.bfloat16)
    output = jnp.einsum("tgrl,lgd->tgrd", rounded, value_rows, preferred_element_type=jnp.float32)
    row_dot = jnp.sum(grad_part.astype(jnp.float32) * output, axis=-1, keepdims=True)
    grad_weights = jnp.einsum(
        "tgrd,lgd->tgrl", grad_part, value_rows, preferred_element_type=jnp.float32
    )
    grad_scores = (weights * (grad_weights - row_dot)).astype(jnp.bfloat16)
    query_grad = (
        jnp.einsum("tgrl,lgd->tgrd", grad_scores, key_rows, preferred_element_type=jnp.float32)
        * scaling
    )
    key_grad = (
        jnp.einsum("tgrl,tgrd->lgd", grad_scores, query_part, preferred_element_type=jnp.float32)
        * scaling
    )
    value_grad = jnp.einsum(
        "tgrl,tgrd->lgd", rounded, grad_part, preferred_element_type=jnp.float32
    )
    return (query_grad, key_grad, value_grad)


def run_attention(query_stack, grad_stack, key_stack, value_stack, allowed_stack):

    def attend_half(items):
        return attend(items[0], items[1], items[2], items[3], items[4])

    return lax.map(attend_half, (query_stack, grad_stack, key_stack, value_stack, allowed_stack))


def on_device(
    projected_queries,
    projected_keys,
    projected_values,
    output_gradient,
    normed_layer_input,
    segment,
    query_adapter_down,
    query_adapter_up,
    value_adapter_down,
    value_adapter_up,
):
    tok_rows = projected_queries.shape[0]
    query_width = projected_queries.shape[2]
    key_width = projected_keys.shape[2]
    key_value_heads = key_width // HEAD_SIZE
    head_repeat = QUERY_HEADS // KEY_VALUE_HEADS
    group_devs = GROUP // tok_rows
    half_span = group_devs // 2
    device = lax.axis_index("ctx")
    ctx_count = lax.axis_size("ctx")
    span = group_devs * tok_rows
    row_index = jnp.arange(tok_rows, dtype=jnp.int32)
    own_block = jnp.concatenate(
        [
            projected_keys[:, 0],
            projected_values[:, 0],
            projected_keys[:, 1],
            projected_values[:, 1],
        ],
        axis=1,
    )
    collected = jnp.zeros((group_devs,) + own_block.shape, own_block.dtype)
    collected = lax.dynamic_update_index_in_dim(collected, own_block, 0, 0)

    def forward_step(distance, state_pair):
        current, gathered = state_pair
        current = shifted(current, "ctx", 1)
        gathered = lax.dynamic_update_index_in_dim(gathered, current, distance, 0)
        return (current, gathered)

    current, collected = lax.fori_loop(1, group_devs, forward_step, (own_block, collected))
    table = collected.reshape(span, 4, key_value_heads, HEAD_SIZE)
    key_stack = jnp.stack([table[:, 0], table[:, 2]])
    value_stack = jnp.stack([table[:, 1], table[:, 3]])
    query_stack = jnp.stack([projected_queries[:, 0], projected_queries[:, 1]]).reshape(
        2, tok_rows, key_value_heads, head_repeat, HEAD_SIZE
    )
    grad_stack = jnp.stack([output_gradient[:, 0], output_gradient[:, 1]]).reshape(
        2, tok_rows, key_value_heads, head_repeat, HEAD_SIZE
    )
    distance_of = jnp.repeat(jnp.arange(group_devs, dtype=jnp.int32), tok_rows)
    row_of = jnp.tile(row_index, group_devs)
    source_rows = (device - distance_of) % ctx_count * tok_rows + row_of
    key_ids = jnp.take(segment, source_rows)
    query_ids = lax.dynamic_slice_in_dim(segment, device * tok_rows, tok_rows)
    frame_positions = jnp.stack([device % group_devs, (device - half_span) % group_devs])
    key_pos = (frame_positions[:, None] - distance_of[None, :]) * tok_rows + row_of[None, :]
    query_pos = frame_positions[:, None] * tok_rows + row_index[None, :]
    visible = distance_of[None, :] <= frame_positions[:, None]
    allowed_stack = (
        visible[:, None, :]
        & (key_pos[:, None, :] <= query_pos[:, :, None])
        & (key_ids[None, None, :] == query_ids[None, :, None])
    )
    query_grad, key_grad, value_grad = run_attention(
        query_stack, grad_stack, key_stack, value_stack, allowed_stack
    )
    partials = jnp.stack([key_grad[0], value_grad[0], key_grad[1], value_grad[1]], axis=1).reshape(
        group_devs, tok_rows, 4 * key_width
    )

    def backward_step(turn_index, carried):
        carried = shifted(carried, "ctx", -1)
        return carried + lax.dynamic_index_in_dim(
            partials, group_devs - 2 - turn_index, 0, keepdims=False
        )

    own_grads = lax.fori_loop(0, group_devs - 1, backward_step, partials[group_devs - 1]).astype(
        jnp.bfloat16
    )
    query_rounded = query_grad.reshape(2, tok_rows, query_width).astype(jnp.bfloat16)
    grad_query = jnp.stack([query_rounded[0], query_rounded[1]], axis=1)
    grad_key = jnp.stack(
        [own_grads[:, :key_width], own_grads[:, 2 * key_width : 3 * key_width]], axis=1
    )
    grad_value = jnp.stack(
        [own_grads[:, key_width : 2 * key_width], own_grads[:, 3 * key_width :]], axis=1
    )
    adapter_input = lax.psum(
        (
            jnp.dot(normed_layer_input, query_adapter_down.T, preferred_element_type=jnp.float32),
            jnp.dot(normed_layer_input, value_adapter_down.T, preferred_element_type=jnp.float32),
        ),
        "fsdp",
    )
    query_down_part = adapter_input[0].astype(jnp.bfloat16)
    value_down_part = adapter_input[1].astype(jnp.bfloat16)
    query_flattened_rows = grad_query.reshape(tok_rows, -1)
    value_flattened_rows = grad_value.reshape(tok_rows, -1)
    adapter_rank_rows = query_adapter_up.shape[0]
    adapter_output = lax.psum(
        (
            jnp.dot(
                query_flattened_rows,
                query_adapter_up.reshape(adapter_rank_rows, -1).T,
                preferred_element_type=jnp.float32,
            ),
            jnp.dot(
                value_flattened_rows,
                value_adapter_up.reshape(adapter_rank_rows, -1).T,
                preferred_element_type=jnp.float32,
            ),
        ),
        "fsdp",
    )
    query_up_part = adapter_output[0].astype(jnp.bfloat16)
    value_up_part = adapter_output[1].astype(jnp.bfloat16)
    local_down_query = jnp.dot(
        query_up_part.T, normed_layer_input, preferred_element_type=jnp.float32
    )
    local_up_query = jnp.dot(
        query_down_part.T, query_flattened_rows, preferred_element_type=jnp.float32
    ).reshape(adapter_rank_rows, 2, -1)
    local_down_value = jnp.dot(
        value_up_part.T, normed_layer_input, preferred_element_type=jnp.float32
    )
    local_up_value = jnp.dot(
        value_down_part.T, value_flattened_rows, preferred_element_type=jnp.float32
    ).reshape(adapter_rank_rows, 2, -1)
    gradient_totals = lax.psum(
        (local_down_query, local_up_query, local_down_value, local_up_value), "ctx"
    )
    return (
        grad_query,
        grad_key,
        grad_value,
        adapter_scale * gradient_totals[0],
        adapter_scale * gradient_totals[1],
        adapter_scale * gradient_totals[2],
        adapter_scale * gradient_totals[3],
    )


def solution(mesh):
    in_specs = (
        P(("rep", "ctx"), None, "fsdp"),
        P(("rep", "ctx"), None, "fsdp"),
        P(("rep", "ctx"), None, "fsdp"),
        P(("rep", "ctx"), None, "fsdp"),
        P(("rep", "ctx"), "fsdp"),
        P("rep"),
        P(None, "fsdp"),
        P(None, None, "fsdp"),
        P(None, "fsdp"),
        P(None, None, "fsdp"),
    )
    out_specs = (
        P(("rep", "ctx"), None, "fsdp"),
        P(("rep", "ctx"), None, "fsdp"),
        P(("rep", "ctx"), None, "fsdp"),
        P("rep", "fsdp"),
        P("rep", None, "fsdp"),
        P("rep", "fsdp"),
        P("rep", None, "fsdp"),
    )
    return jax.shard_map(
        on_device, mesh=mesh, in_specs=in_specs, out_specs=out_specs, check_vma=False
    )
```

profile of v0, /device:TPU:0, one launch (start us, length us, event | category | flops | bytes accessed | tf_op | source)
XLA Modules:
  0.0 456.9 jit_solution(11667846638343664478)
XLA Ops:
  8.5 5.7 %gather_fusion = s32[1024]{0:T(1024)S(1)} fusion(s32[4096]{0:T(1024)} %param.21, s32[1024]{0:T(1024)S(1)} %broadcast_clamp_fusion), kind=kCustom, calls=%fused_computation | custom fusion | bytes 12288 | tf_op jit(solution)/shard_map/jit(_take)/gather | solution.py:113
  16.3 72.0 %while.44 = (s32[]{:T(128)}, bf16[128,1024]{1,0:T(8,128)(2,1)S(1)}, bf16[8,128,1024]{2,1,0:T(8,128)(2,1)}, s32[]{:T(128)}, s32[]{:T(128)}, /*index=5*/s32[]{:T(128)}) while((s32[]{:T(128)}, bf16[128,1024]{1,0:T(8,128)(2,1)S(1)}, bf16[8,128,1024]{2,1,0:T(8,128)(2,1)}, s32[]{:T(128)}, s32[]{:T(128)}, /*index=5*/s32[]{:T(128)}) %tuple.105), condition=%wide.region_1.2_spmd, body=%wide.region_0.1_spmd.sunk | while | flops 5 | bytes 2097307 | solution.py:100
  16.8 10.0 %collective-permute-done = bf16[128,1024]{1,0:T(8,128)(2,1)S(1)} collective-permute-done((bf16[128,1024]{1,0:T(8,128)(2,1)S(1)}, bf16[128,1024]{1,0:T(8,128)(2,1)S(1)}, u32[]{:S(2)}, u32[]{:S(2)}) %collective-permute-start) | collective-permute-done | bytes 262176 | tf_op jit(solution)/shard_map/while/body/eval_jaxpr/ppermute | solution.py:17
  27.5 9.4 %collective-permute-done = bf16[128,1024]{1,0:T(8,128)(2,1)S(1)} collective-permute-done((bf16[128,1024]{1,0:T(8,128)(2,1)S(1)}, bf16[128,1024]{1,0:T(8,128)(2,1)S(1)}, u32[]{:S(2)}, u32[]{:S(2)}) %collective-permute-start) | collective-permute-done | bytes 262176 | tf_op jit(solution)/shard_map/while/body/eval_jaxpr/ppermute | solution.py:17
  37.7 9.4 %collective-permute-done = bf16[128,1024]{1,0:T(8,128)(2,1)S(1)} collective-permute-done((bf16[128,1024]{1,0:T(8,128)(2,1)S(1)}, bf16[128,1024]{1,0:T(8,128)(2,1)S(1)}, u32[]{:S(2)}, u32[]{:S(2)}) %collective-permute-start) | collective-permute-done | bytes 262176 | tf_op jit(solution)/shard_map/while/body/eval_jaxpr/ppermute | solution.py:17
  47.8 9.4 %collective-permute-done = bf16[128,1024]{1,0:T(8,128)(2,1)S(1)} collective-permute-done((bf16[128,1024]{1,0:T(8,128)(2,1)S(1)}, bf16[128,1024]{1,0:T(8,128)(2,1)S(1)}, u32[]{:S(2)}, u32[]{:S(2)}) %collective-permute-start) | collective-permute-done | bytes 262176 | tf_op jit(solution)/shard_map/while/body/eval_jaxpr/ppermute | solution.py:17
  57.9 9.4 %collective-permute-done = bf16[128,1024]{1,0:T(8,128)(2,1)S(1)} collective-permute-done((bf16[128,1024]{1,0:T(8,128)(2,1)S(1)}, bf16[128,1024]{1,0:T(8,128)(2,1)S(1)}, u32[]{:S(2)}, u32[]{:S(2)}) %collective-permute-start) | collective-permute-done | bytes 262176 | tf_op jit(solution)/shard_map/while/body/eval_jaxpr/ppermute | solution.py:17
  68.1 9.4 %collective-permute-done = bf16[128,1024]{1,0:T(8,128)(2,1)S(1)} collective-permute-done((bf16[128,1024]{1,0:T(8,128)(2,1)S(1)}, bf16[128,1024]{1,0:T(8,128)(2,1)S(1)}, u32[]{:S(2)}, u32[]{:S(2)}) %collective-permute-start) | collective-permute-done | bytes 262176 | tf_op jit(solution)/shard_map/while/body/eval_jaxpr/ppermute | solution.py:17
  78.2 9.4 %collective-permute-done = bf16[128,1024]{1,0:T(8,128)(2,1)S(1)} collective-permute-done((bf16[128,1024]{1,0:T(8,128)(2,1)S(1)}, bf16[128,1024]{1,0:T(8,128)(2,1)S(1)}, u32[]{:S(2)}, u32[]{:S(2)}) %collective-permute-start) | collective-permute-done | bytes 262176 | tf_op jit(solution)/shard_map/while/body/eval_jaxpr/ppermute | solution.py:17
  130.9 60.9 %while.45 = (s32[]{:T(128)}, bf16[2,128,2,8,128]{1,4,3,2,0:T(8,128)(2,1)}, f32[2,1024,2,128]{1,3,2,0:T(8,128)}, f32[2,1024,2,128]{1,3,2,0:T(8,128)}, bf16[2,1024...) while((s32[]{:T(128)}, ...), condition=%wide.region_6.7_spmd, body=%wide.region_2.6_spmd.sunk | while | flops 3243506688 | bytes 127842224 | solution.py:56
  130.9 7.3 %fusion.134 = (f32[128,2,8]{0,2,1:T(8,128)S(1)}, f32[128,2,8,1024]{0,3,2,1:T(8,128)}) fusion(pred[128,1024]{0,1:T(8,128)(4,1)S(1)} %dynamic-slice_bitcast_fusion.2, bf16[2,128,2,8,128]{1,4,3,2,0:T(8,128)(2,1)} %get-tuple-element.478, s32[]{:T(128)} %get-tuple-element.462, bf16[2,1024,2,128]{1,3,2,0:T(8,128)(2,1)S(1)} %get-tuple-element.476), kind=kOutput, calls=%fused_computation.126.clone.1 | convolution fusion | flops 545260544 | bytes 9577472 | tf_op jit(solution)/shard_map/while/body/eval_jaxpr/sub | solution.py:28
  138.2 6.5 %fusion.135 = bf16[128,2,8,1024]{0,3,2,1:T(8,128)(2,1)} fusion(f32[128,2,8,1024]{0,3,2,1:T(8,128)} %get-tuple-element.429, f32[128,2,8]{0,2,1:T(8,128)S(1)} %get-tuple-element.430), kind=kLoop, calls=%fused_computation.13.clone.1 | loop fusion | flops 4194304 | bytes 12591104 | tf_op jit(solution)/shard_map/while/body/eval_jaxpr/convert_element_type | solution.py:30
  161.4 7.3 %fusion.134 = (f32[128,2,8]{0,2,1:T(8,128)S(1)}, f32[128,2,8,1024]{0,3,2,1:T(8,128)}) fusion(pred[128,1024]{0,1:T(8,128)(4,1)S(1)} %dynamic-slice_bitcast_fusion.2, bf16[2,128,2,8,128]{1,4,3,2,0:T(8,128)(2,1)} %get-tuple-element.478, s32[]{:T(128)} %get-tuple-element.462, bf16[2,1024,2,128]{1,3,2,0:T(8,128)(2,1)S(1)} %get-tuple-element.476), kind=kOutput, calls=%fused_computation.126.clone.1 | convolution fusion | flops 545260544 | bytes 9577472 | tf_op jit(solution)/shard_map/while/body/eval_jaxpr/sub | solution.py:28
  168.7 6.5 %fusion.135 = bf16[128,2,8,1024]{0,3,2,1:T(8,128)(2,1)} fusion(f32[128,2,8,1024]{0,3,2,1:T(8,128)} %get-tuple-element.429, f32[128,2,8]{0,2,1:T(8,128)S(1)} %get-tuple-element.430), kind=kLoop, calls=%fused_computation.13.clone.1 | loop fusion | flops 4194304 | bytes 12591104 | tf_op jit(solution)/shard_map/while/body/eval_jaxpr/convert_element_type | solution.py:30
  180.0 4.5 fusion.137
  199.8 95.4 %while.46 = (s32[]{:T(128)}, f32[128,1024]{1,0:T(8,128)}, f32[8,128,1024]{1,0,2:T(8,128)}, s32[]{:T(128)}, s32[]{:T(128)}, /*index=5*/s32[]{:T(128)}, s32[]{:T(128)}) while((s32[]{:T(128)}, f32[128,1024]{1,0:T(8,128)}, f32[8,128,1024]{1,0,2:T(8,128)}, s32[]{:T(128)}, s32[]{:T(128)}, /*index=5*/s32[]{:T(128)}, s32[]{:T(128)}) %tuple.117), condition=%wide.region_8.9_spmd, body=%wide.region_7.8_spmd.sunk | while | flops 131078 | bytes 5767335 | solution.py:137
  208.7 5.5 %collective-permute-start.1 = (f32[128,1024]{1,0:T(8,128)}, f32[128,1024]{1,0:T(8,128)}, u32[]{:S(2)}, u32[]{:S(2)}) collective-permute-start(f32[128,1024]{1,0:T(8,128)} %get-tuple-element.490), channel_id=1, source_target_pairs={{0,31},{1,0},{2,1},{3,2},{4,3},{5,4},{6,5},{7,6},{8,7},{9,8},{10,9... | collective-permute-start | bytes 1572872 | tf_op jit(solution)/shard_map/while/body/eval_jaxpr/ppermute | solution.py:17
  223.2 5.5 %collective-permute-start.1 = (f32[128,1024]{1,0:T(8,128)}, f32[128,1024]{1,0:T(8,128)}, u32[]{:S(2)}, u32[]{:S(2)}) collective-permute-start(f32[128,1024]{1,0:T(8,128)} %get-tuple-element.490), channel_id=1, source_target_pairs={{0,31},{1,0},{2,1},{3,2},{4,3},{5,4},{6,5},{7,6},{8,7},{9,8},{10,9... | collective-permute-start | bytes 1572872 | tf_op jit(solution)/shard_map/while/body/eval_jaxpr/ppermute | solution.py:17
  237.6 5.5 %collective-permute-start.1 = (f32[128,1024]{1,0:T(8,128)}, f32[128,1024]{1,0:T(8,128)}, u32[]{:S(2)}, u32[]{:S(2)}) collective-permute-start(f32[128,1024]{1,0:T(8,128)} %get-tuple-element.490), channel_id=1, source_target_pairs={{0,31},{1,0},{2,1},{3,2},{4,3},{5,4},{6,5},{7,6},{8,7},{9,8},{10,9... | collective-permute-start | bytes 1572872 | tf_op jit(solution)/shard_map/while/body/eval_jaxpr/ppermute | solution.py:17
  252.0 5.5 %collective-permute-start.1 = (f32[128,1024]{1,0:T(8,128)}, f32[128,1024]{1,0:T(8,128)}, u32[]{:S(2)}, u32[]{:S(2)}) collective-permute-start(f32[128,1024]{1,0:T(8,128)} %get-tuple-element.490), channel_id=1, source_target_pairs={{0,31},{1,0},{2,1},{3,2},{4,3},{5,4},{6,5},{7,6},{8,7},{9,8},{10,9... | collective-permute-start | bytes 1572872 | tf_op jit(solution)/shard_map/while/body/eval_jaxpr/ppermute | solution.py:17
  266.4 5.5 %collective-permute-start.1 = (f32[128,1024]{1,0:T(8,128)}, f32[128,1024]{1,0:T(8,128)}, u32[]{:S(2)}, u32[]{:S(2)}) collective-permute-start(f32[128,1024]{1,0:T(8,128)} %get-tuple-element.490), channel_id=1, source_target_pairs={{0,31},{1,0},{2,1},{3,2},{4,3},{5,4},{6,5},{7,6},{8,7},{9,8},{10,9... | collective-permute-start | bytes 1572872 | tf_op jit(solution)/shard_map/while/body/eval_jaxpr/ppermute | solution.py:17
  280.8 5.5 %collective-permute-start.1 = (f32[128,1024]{1,0:T(8,128)}, f32[128,1024]{1,0:T(8,128)}, u32[]{:S(2)}, u32[]{:S(2)}) collective-permute-start(f32[128,1024]{1,0:T(8,128)} %get-tuple-element.490), channel_id=1, source_target_pairs={{0,31},{1,0},{2,1},{3,2},{4,3},{5,4},{6,5},{7,6},{8,7},{9,8},{10,9... | collective-permute-start | bytes 1572872 | tf_op jit(solution)/shard_map/while/body/eval_jaxpr/ppermute | solution.py:17
  315.5 38.7 %psum.31 = f32[16,2,256]{2,0,1:T(8,128)S(1)} all-reduce(f32[16,2,256]{2,0,1:T(8,128)S(1)} %fusion.65), channel_id=1, replica_groups=mesh['rep'=1,'ctx'=32,'fsdp'=1] {'ctx'}, use_global_device_ids=true, to_apply=%region_12.13 | all-reduce | flops 8192 | bytes 65536 | tf_op jit(solution)/shard_map/psum | solution.py:189
  355.7 88.8 %all-reduce.4.cloned.1.call-done = (f32[16,8192]{1,0:T(8,128)}, f32[16,2,2048]{2,0,1:T(8,128)}, f32[16,8192]{1,0:T(8,128)}) async-done(((f32[16,8192]{1,0:T(8,128)}, f32[16,2,2048]{2,0,1:T(8,128)}, f32[16,8192]{1,0:T(8,128)}), (f32[16,8192]{1,0:T(8,128)}, f32[16,2,2048]{2,0,1:T(8,128)}, f32[16,8192]{1,0:T(8,128)})) %all-reduce.4.cloned.1.call-update) | async-done | bytes 1310736 | tf_op jit(solution)/shard_map/psum | solution.py:189
  (195 shorter events, 177.5 us)
Async XLA Ops:
  7.2 295.3 %copy-start = (bf16[128,8192]{1,0:T(8,128)(2,1)S(1)}, bf16[128,8192]{1,0:T(8,128)(2,1)}, u32[]{:S(2)}) copy-start(bf16[128,8192]{1,0:T(8,128)(2,1)} %param.20) | copy-start | bytes 6291460
  7.2 7.0 %copy-start.16 = (bf16[128,2,256]{2,1,0:T(2,128)(2,1)S(1)}, bf16[128,2,256]{2,1,0:T(2,128)(2,1)}, u32[]{:S(2)}) copy-start(bf16[128,2,256]{2,1,0:T(2,128)(2,1)} %param.18) | copy-start | bytes 393220
  7.2 7.2 %copy-start.17 = (bf16[128,2,256]{2,1,0:T(2,128)(2,1)S(1)}, bf16[128,2,256]{2,1,0:T(2,128)(2,1)}, u32[]{:S(2)}) copy-start(bf16[128,2,256]{2,1,0:T(2,128)(2,1)} %param.17) | copy-start | bytes 393220
  7.2 437.3 %all-reduce.4.cloned.1.call-start = ((), (), s32[]{:S(2)}) async-start(), calls=%async_computation | async-start | bytes 2621440 | tf_op jit(solution)/shard_map/psum | solution.py:189
  16.3 10.4 %collective-permute-start = (bf16[128,1024]{1,0:T(8,128)(2,1)S(1)}, bf16[128,1024]{1,0:T(8,128)(2,1)S(1)}, u32[]{:S(2)}, u32[]{:S(2)}) collective-permute-start(bf16[128,1024]{1,0:T(8,128)(2,1)S(1)} %get-tuple-element.441), channel_id=1, source_target_pairs={{0,1},{1,2},{2,3},{3,4},{4,5},{5,6},{6,7},{7,8},{8,9},{9,10},{10,1... | collective-permute-start | bytes 786440 | tf_op jit(solution)/shard_map/while/body/eval_jaxpr/ppermute | solution.py:17
  27.5 9.4 %collective-permute-start = (bf16[128,1024]{1,0:T(8,128)(2,1)S(1)}, bf16[128,1024]{1,0:T(8,128)(2,1)S(1)}, u32[]{:S(2)}, u32[]{:S(2)}) collective-permute-start(bf16[128,1024]{1,0:T(8,128)(2,1)S(1)} %get-tuple-element.441), channel_id=1, source_target_pairs={{0,1},{1,2},{2,3},{3,4},{4,5},{5,6},{6,7},{7,8},{8,9},{9,10},{10,1... | collective-permute-start | bytes 786440 | tf_op jit(solution)/shard_map/while/body/eval_jaxpr/ppermute | solution.py:17
  37.6 9.4 %collective-permute-start = (bf16[128,1024]{1,0:T(8,128)(2,1)S(1)}, bf16[128,1024]{1,0:T(8,128)(2,1)S(1)}, u32[]{:S(2)}, u32[]{:S(2)}) collective-permute-start(bf16[128,1024]{1,0:T(8,128)(2,1)S(1)} %get-tuple-element.441), channel_id=1, source_target_pairs={{0,1},{1,2},{2,3},{3,4},{4,5},{5,6},{6,7},{7,8},{8,9},{9,10},{10,1... | collective-permute-start | bytes 786440 | tf_op jit(solution)/shard_map/while/body/eval_jaxpr/ppermute | solution.py:17
  47.8 9.4 %collective-permute-start = (bf16[128,1024]{1,0:T(8,128)(2,1)S(1)}, bf16[128,1024]{1,0:T(8,128)(2,1)S(1)}, u32[]{:S(2)}, u32[]{:S(2)}) collective-permute-start(bf16[128,1024]{1,0:T(8,128)(2,1)S(1)} %get-tuple-element.441), channel_id=1, source_target_pairs={{0,1},{1,2},{2,3},{3,4},{4,5},{5,6},{6,7},{7,8},{8,9},{9,10},{10,1... | collective-permute-start | bytes 786440 | tf_op jit(solution)/shard_map/while/body/eval_jaxpr/ppermute | solution.py:17
  57.9 9.4 %collective-permute-start = (bf16[128,1024]{1,0:T(8,128)(2,1)S(1)}, bf16[128,1024]{1,0:T(8,128)(2,1)S(1)}, u32[]{:S(2)}, u32[]{:S(2)}) collective-permute-start(bf16[128,1024]{1,0:T(8,128)(2,1)S(1)} %get-tuple-element.441), channel_id=1, source_target_pairs={{0,1},{1,2},{2,3},{3,4},{4,5},{5,6},{6,7},{7,8},{8,9},{9,10},{10,1... | collective-permute-start | bytes 786440 | tf_op jit(solution)/shard_map/while/body/eval_jaxpr/ppermute | solution.py:17
  68.1 9.4 %collective-permute-start = (bf16[128,1024]{1,0:T(8,128)(2,1)S(1)}, bf16[128,1024]{1,0:T(8,128)(2,1)S(1)}, u32[]{:S(2)}, u32[]{:S(2)}) collective-permute-start(bf16[128,1024]{1,0:T(8,128)(2,1)S(1)} %get-tuple-element.441), channel_id=1, source_target_pairs={{0,1},{1,2},{2,3},{3,4},{4,5},{5,6},{6,7},{7,8},{8,9},{9,10},{10,1... | collective-permute-start | bytes 786440 | tf_op jit(solution)/shard_map/while/body/eval_jaxpr/ppermute | solution.py:17
  78.2 9.4 %collective-permute-start = (bf16[128,1024]{1,0:T(8,128)(2,1)S(1)}, bf16[128,1024]{1,0:T(8,128)(2,1)S(1)}, u32[]{:S(2)}, u32[]{:S(2)}) collective-permute-start(bf16[128,1024]{1,0:T(8,128)(2,1)S(1)} %get-tuple-element.441), channel_id=1, source_target_pairs={{0,1},{1,2},{2,3},{3,4},{4,5},{5,6},{6,7},{7,8},{8,9},{9,10},{10,1... | collective-permute-start | bytes 786440 | tf_op jit(solution)/shard_map/while/body/eval_jaxpr/ppermute | solution.py:17
  92.8 11.7 %copy-start.8 = (bf16[128,2,2048]{2,1,0:T(2,128)(2,1)S(1)}, bf16[128,2,2048]{2,1,0:T(2,128)(2,1)}, u32[]{:S(2)}) copy-start(bf16[128,2,2048]{2,1,0:T(2,128)(2,1)} %param.16) | copy-start | bytes 3145732
  106.9 7.1 %copy-start.9 = (bf16[128,2,2048]{2,1,0:T(2,128)(2,1)S(1)}, bf16[128,2,2048]{2,1,0:T(2,128)(2,1)}, u32[]{:S(2)}) copy-start(bf16[128,2,2048]{2,1,0:T(2,128)(2,1)} %param.19) | copy-start | bytes 3145732
  130.9 7.3 %copy-start.4 = (bf16[2,1024,2,128]{1,3,2,0:T(8,128)(2,1)}, bf16[2,1024,2,128]{1,3,2,0:T(8,128)(2,1)S(1)}, u32[]{:S(2)}) copy-start(bf16[2,1024,2,128]{1,3,2,0:T(8,128)(2,1)S(1)} %get-tuple-element.476) | copy-start | bytes 3145732 | tf_op jit(solution)/shard_map/while
  161.4 7.3 %copy-start.4 = (bf16[2,1024,2,128]{1,3,2,0:T(8,128)(2,1)}, bf16[2,1024,2,128]{1,3,2,0:T(8,128)(2,1)S(1)}, u32[]{:S(2)}) copy-start(bf16[2,1024,2,128]{1,3,2,0:T(8,128)(2,1)S(1)} %get-tuple-element.476) | copy-start | bytes 3145732 | tf_op jit(solution)/shard_map/while
  168.7 6.5 %copy-start.2 = (bf16[2,128,2,8,128]{1,4,3,2,0:T(8,128)(2,1)S(1)}, bf16[2,128,2,8,128]{1,4,3,2,0:T(8,128)(2,1)}, u32[]{:S(2)}) copy-start(bf16[2,128,2,8,128]{1,4,3,2,0:T(8,128)(2,1)} %get-tuple-element.480) | copy-start | bytes 3145732 | tf_op jit(solution)/shard_map/while
  199.8 7.0 %collective-permute-start.1 = (f32[128,1024]{1,0:T(8,128)}, f32[128,1024]{1,0:T(8,128)}, u32[]{:S(2)}, u32[]{:S(2)}) collective-permute-start(f32[128,1024]{1,0:T(8,128)} %get-tuple-element.490), channel_id=1, source_target_pairs={{0,31},{1,0},{2,1},{3,2},{4,3},{5,4},{6,5},{7,6},{8,7},{9,8},{10,9... | collective-permute-start | bytes 1572872 | tf_op jit(solution)/shard_map/while/body/eval_jaxpr/ppermute | solution.py:17
  208.7 12.5 %collective-permute-start.1 = (f32[128,1024]{1,0:T(8,128)}, f32[128,1024]{1,0:T(8,128)}, u32[]{:S(2)}, u32[]{:S(2)}) collective-permute-start(f32[128,1024]{1,0:T(8,128)} %get-tuple-element.490), channel_id=1, source_target_pairs={{0,31},{1,0},{2,1},{3,2},{4,3},{5,4},{6,5},{7,6},{8,7},{9,8},{10,9... | collective-permute-start | bytes 1572872 | tf_op jit(solution)/shard_map/while/body/eval_jaxpr/ppermute | solution.py:17
  223.2 12.5 %collective-permute-start.1 = (f32[128,1024]{1,0:T(8,128)}, f32[128,1024]{1,0:T(8,128)}, u32[]{:S(2)}, u32[]{:S(2)}) collective-permute-start(f32[128,1024]{1,0:T(8,128)} %get-tuple-element.490), channel_id=1, source_target_pairs={{0,31},{1,0},{2,1},{3,2},{4,3},{5,4},{6,5},{7,6},{8,7},{9,8},{10,9... | collective-permute-start | bytes 1572872 | tf_op jit(solution)/shard_map/while/body/eval_jaxpr/ppermute | solution.py:17
  237.6 12.5 %collective-permute-start.1 = (f32[128,1024]{1,0:T(8,128)}, f32[128,1024]{1,0:T(8,128)}, u32[]{:S(2)}, u32[]{:S(2)}) collective-permute-start(f32[128,1024]{1,0:T(8,128)} %get-tuple-element.490), channel_id=1, source_target_pairs={{0,31},{1,0},{2,1},{3,2},{4,3},{5,4},{6,5},{7,6},{8,7},{9,8},{10,9... | collective-permute-start | bytes 1572872 | tf_op jit(solution)/shard_map/while/body/eval_jaxpr/ppermute | solution.py:17
  252.0 12.5 %collective-permute-start.1 = (f32[128,1024]{1,0:T(8,128)}, f32[128,1024]{1,0:T(8,128)}, u32[]{:S(2)}, u32[]{:S(2)}) collective-permute-start(f32[128,1024]{1,0:T(8,128)} %get-tuple-element.490), channel_id=1, source_target_pairs={{0,31},{1,0},{2,1},{3,2},{4,3},{5,4},{6,5},{7,6},{8,7},{9,8},{10,9... | collective-permute-start | bytes 1572872 | tf_op jit(solution)/shard_map/while/body/eval_jaxpr/ppermute | solution.py:17
  266.4 12.5 %collective-permute-start.1 = (f32[128,1024]{1,0:T(8,128)}, f32[128,1024]{1,0:T(8,128)}, u32[]{:S(2)}, u32[]{:S(2)}) collective-permute-start(f32[128,1024]{1,0:T(8,128)} %get-tuple-element.490), channel_id=1, source_target_pairs={{0,31},{1,0},{2,1},{3,2},{4,3},{5,4},{6,5},{7,6},{8,7},{9,8},{10,9... | collective-permute-start | bytes 1572872 | tf_op jit(solution)/shard_map/while/body/eval_jaxpr/ppermute | solution.py:17
  280.8 12.5 %collective-permute-start.1 = (f32[128,1024]{1,0:T(8,128)}, f32[128,1024]{1,0:T(8,128)}, u32[]{:S(2)}, u32[]{:S(2)}) collective-permute-start(f32[128,1024]{1,0:T(8,128)} %get-tuple-element.490), channel_id=1, source_target_pairs={{0,31},{1,0},{2,1},{3,2},{4,3},{5,4},{6,5},{7,6},{8,7},{9,8},{10,9... | collective-permute-start | bytes 1572872 | tf_op jit(solution)/shard_map/while/body/eval_jaxpr/ppermute | solution.py:17
  302.5 6.9 %copy-start.19 = (bf16[16,2,256]{2,1,0:T(2,128)(2,1)S(1)}, bf16[16,2,256]{2,1,0:T(2,128)(2,1)}, u32[]{:S(2)}) copy-start(bf16[16,2,256]{2,1,0:T(2,128)(2,1)} %param.25) | copy-start | bytes 49156
  (22 other events, 75.3 us)
Sparse Core Ops, SparseCore 0:
  310.9 133.5 all-reduce.3
where the time goes:
time: 459 us; the launch traced here: 457 us
  waiting for transfers between devices  184 us (40%)
  local copies, waits for them, and re-layouts  92.1 us (20%)
  matrix products  52.3 us (11%)
  other arithmetic  41.7 us (9%)
  blocking collectives  38.7 us (8%)
  starting transfers between devices  33.5 us (7%)
  between operations  14.4 us (3%)
    ppermute x14, waiting for transfers between devices, shifted(): return lax.ppermute(x, axis, [(i, (i + by) % size) for i in range(size)])  95.1 us
    psum x1, waiting for transfers between devices, on_device(): lax.psum((local_down_query, local_up_query, local_down_value, local_up_va...  88.8 us
    psum x1, blocking collectives, on_device(): lax.psum((local_down_query, local_up_query, local_down_value, local_up_va...  38.7 us
    ppermute x14, starting transfers between devices, shifted(): return lax.ppermute(x, axis, [(i, (i + by) % size) for i in range(size)])  33.5 us
    unnamed x32, local copies, waits for them, and re-layouts  30.3 us
    dynamic_slice x14, local copies, waits for them, and re-layouts, backward_step(): lax.dynamic_index_in_dim(partials, group_devs - 2 - turn_index, 0, keepdi...  20.3 us
    sub x2, matrix products, attend(): weights = jnp.exp(scores - highest)  14.6 us
    add x7, other arithmetic, backward_step(): carried + lax.dynamic_index_in_dim(partials, group_devs - 2 - turn_index,...  13.2 us
  transfers between devices with their start and end apart: 15, of which 15 were waited for; matrix products, arithmetic and copies ran while one was open for 6% of the time, Pallas kernels for 0%

commit v1 on v0

v1 whole, which is shorter than its diff:
```python
import functools
import math

import jax
import jax.numpy as jnp
from jax import lax
from jax.experimental import pallas as pl
from jax.experimental.pallas import tpu as pltpu
from jax.sharding import PartitionSpec as P

MESH = pl.DeviceIdType.MESH
MASKED = -1e30

QUERY_HEADS = 32
KEY_VALUE_HEADS = 4
HEAD_SIZE = 128
GROUP = 1024


adapter_scale = 2.0


def attention_kernel(
    ctx,
    devs,
    q_ref,
    do_ref,
    kv_ref,
    seg_ref,
    dq_ref,
    gkv_ref,
    kv_buf,
    part_send,
    part_recv,
    own_part,
    p_scr,
    ds_scr,
    bias,
    g_send,
    g_recv,
    r_send,
    r_recv,
):
    kv_heads = kv_ref.shape[1]
    tok = kv_ref.shape[2]
    repeat = q_ref.shape[1] // kv_heads
    mid = devs // 2
    scaling = HEAD_SIZE ** (-0.5)
    exponent = scaling * math.log2(math.e)
    me = lax.axis_index("ctx")
    p0 = lax.rem(me, devs)
    small = p0 // mid
    big = 1 - small
    ps = lax.rem(p0, mid)

    def ahead(d):
        return lax.rem(me + d, ctx)

    def behind(d):
        return lax.rem(me + ctx - d, ctx)

    barrier = pltpu.get_barrier_semaphore()
    for d in range(1, devs):
        pl.semaphore_signal(barrier, inc=1, device_id={"ctx": ahead(d)}, device_id_type=MESH)
        pl.semaphore_signal(barrier, inc=1, device_id={"ctx": behind(d)}, device_id_type=MESH)
    pl.semaphore_wait(barrier, 2 * (devs - 1))

    def gather_copy(h, d):
        return pltpu.make_async_remote_copy(
            src_ref=kv_ref.at[h],
            dst_ref=kv_buf.at[h, d],
            send_sem=g_send.at[h, d],
            recv_sem=g_recv.at[h, d],
            device_id={"ctx": ahead(d)},
            device_id_type=MESH,
        )

    def return_copy(h, g, d):
        return pltpu.make_async_remote_copy(
            src_ref=part_send.at[h, g, d],
            dst_ref=part_recv.at[h, g, d],
            send_sem=r_send.at[h, g, d],
            recv_sem=r_recv.at[h, g, d],
            device_id={"ctx": behind(d)},
            device_id_type=MESH,
        )

    for d in range(1, mid):

        @pl.when(ps + d < mid)
        def _():
            gather_copy(small, d).start()

    for d in range(1, devs):

        @pl.when((ps + d >= mid) & (ps + d < devs))
        def _():
            gather_copy(small, d).start()

    for d in range(1, mid):

        @pl.when(ps + d < mid)
        def _():
            gather_copy(big, d).start()

    for h in range(2):
        kv_buf[h, 0] = kv_ref[h]
    for d in range(1, mid):

        @pl.when(d > ps)
        def _():
            kv_buf[small, d] = jnp.zeros(kv_buf.shape[2:], kv_buf.dtype)

        @pl.when(d > ps)
        def _():
            kv_buf[big, mid + d] = jnp.zeros(kv_buf.shape[2:], kv_buf.dtype)

    own_ids = jnp.transpose(
        jnp.broadcast_to(seg_ref[pl.ds(me, 1), :].astype(jnp.float32), (tok, tok))
    )
    rows = lax.broadcasted_iota(jnp.int32, (tok, tok), 0)
    columns = lax.broadcasted_iota(jnp.int32, (tok, tok), 1)
    for d in range(devs):
        ids = seg_ref[pl.ds(behind(d), 1), :].astype(jnp.float32)
        block = jnp.where(own_ids == ids, 0.0, MASKED)
        if d == 0:
            block = jnp.where(columns <= rows, block, MASKED)
        bias[:, d * tok : (d + 1) * tok] = block

    def attend(h, slots, limit):
        keys = slots * tok

        def head_group(g, carry):
            k = kv_buf[h, :slots, g, :, :HEAD_SIZE].reshape(keys, HEAD_SIZE)
            v = kv_buf[h, :slots, g, :, HEAD_SIZE:].reshape(keys, HEAD_SIZE)

            def one_head(r, inner):
                q = q_ref[h, g * repeat + r]
                do = do_ref[h, g * repeat + r]
                s = lax.dot_general(
                    q, k, (((1,), (1,)), ((), ())), preferred_element_type=jnp.float32
                )
                dp = lax.dot_general(
                    do, v, (((1,), (1,)), ((), ())), preferred_element_type=jnp.float32
                )
                at = lax.broadcasted_iota(jnp.int32, (1, keys), 1)
                reach = jnp.where(at < limit * tok, 0.0, MASKED)
                t = s * exponent + (bias[:, :keys] + reach)
                e = jnp.exp2(t - jnp.max(t, axis=1, keepdims=True))
                w = e * (1.0 / jnp.sum(e, axis=1, keepdims=True))
                low = w.astype(jnp.bfloat16)
                dot = jnp.sum(low.astype(jnp.float32) * dp, axis=1, keepdims=True)
                ds = (w * (dp - dot)).astype(jnp.bfloat16)
                at_row = pl.multiple_of(r * tok, tok)
                p_scr[pl.ds(at_row, tok), :keys] = low
                ds_scr[pl.ds(at_row, tok), :keys] = ds
                dq = jnp.dot(ds, k, preferred_element_type=jnp.float32) * scaling
                dq_ref[h, g * repeat + r] = dq.astype(jnp.bfloat16)
                return inner

            lax.fori_loop(0, repeat, one_head, 0, unroll=2)
            q_all = q_ref[h, pl.ds(g * repeat, repeat)].reshape(repeat * tok, HEAD_SIZE)
            do_all = do_ref[h, pl.ds(g * repeat, repeat)].reshape(repeat * tok, HEAD_SIZE)
            dk = lax.dot_general(
                q_all,
                ds_scr[:, :keys],
                (((0,), (0,)), ((), ())),
                preferred_element_type=jnp.float32,
            )
            dv = lax.dot_general(
                do_all,
                p_scr[:, :keys],
                (((0,), (0,)), ((), ())),
                preferred_element_type=jnp.float32,
            )
            for d in range(slots):
                dk_block = jnp.transpose(dk[:, d * tok : (d + 1) * tok]) * scaling
                dv_block = jnp.transpose(dv[:, d * tok : (d + 1) * tok])
                if d == 0:
                    own_part[h, g, :, :HEAD_SIZE] = dk_block
                    own_part[h, g, :, HEAD_SIZE:] = dv_block
                else:
                    part_send[h, g, d, :, :HEAD_SIZE] = dk_block.astype(jnp.bfloat16)
                    part_send[h, g, d, :, HEAD_SIZE:] = dv_block.astype(jnp.bfloat16)
            for d in range(1, slots):

                @pl.when(d < limit)
                def _():
                    return_copy(h, g, d).start()

            return carry

        lax.fori_loop(0, kv_heads, head_group, 0)

    for d in range(1, mid):

        @pl.when(d <= ps)
        def _():
            gather_copy(small, d).wait_recv()

    attend(small, mid, ps + 1)

    for d in range(1, devs):

        @pl.when(d <= ps + mid)
        def _():
            gather_copy(big, d).wait_recv()

    attend(big, devs, ps + mid + 1)

    for d in range(1, devs):
        for g in range(kv_heads):

            @pl.when(ps + d < devs)
            def _():
                return_copy(small, g, d).wait_recv()
                own_part[small, g] = own_part[small, g] + part_recv[small, g, d].astype(
                    jnp.float32
                )

    for d in range(1, mid):
        for g in range(kv_heads):

            @pl.when(ps + d < mid)
            def _():
                return_copy(big, g, d).wait_recv()
                own_part[big, g] = own_part[big, g] + part_recv[big, g, d].astype(jnp.float32)

    gkv_ref[...] = own_part[...].astype(jnp.bfloat16)

    for d in range(1, devs):

        @pl.when(ps + d < devs)
        def _():
            gather_copy(small, d).wait_send()

        @pl.when(d <= ps + mid)
        def _():
            for g in range(kv_heads):
                return_copy(big, g, d).wait_send()

    for d in range(1, mid):

        @pl.when(ps + d < mid)
        def _():
            gather_copy(big, d).wait_send()

        @pl.when(d <= ps)
        def _():
            for g in range(kv_heads):
                return_copy(small, g, d).wait_send()


def attention_backward(q, do, kv, seg, devs):
    heads, tok = q.shape[1], q.shape[2]
    kv_heads = kv.shape[1]
    repeat = heads // kv_heads
    ctx = lax.axis_size("ctx")
    bf16, f32 = jnp.bfloat16, jnp.float32
    pair = 2 * HEAD_SIZE
    vmem = pl.BlockSpec(memory_space=pltpu.VMEM)
    return pl.pallas_call(
        functools.partial(attention_kernel, ctx, devs),
        out_shape=(
            jax.ShapeDtypeStruct(q.shape, bf16),
            jax.ShapeDtypeStruct(kv.shape, bf16),
        ),
        in_specs=[vmem] * 4,
        out_specs=(vmem, vmem),
        scratch_shapes=[
            pltpu.VMEM((2, devs, kv_heads, tok, pair), bf16),
            pltpu.VMEM((2, kv_heads, devs, tok, pair), bf16),
            pltpu.VMEM((2, kv_heads, devs, tok, pair), bf16),
            pltpu.VMEM((2, kv_heads, tok, pair), f32),
            pltpu.VMEM((repeat * tok, devs * tok), bf16),
            pltpu.VMEM((repeat * tok, devs * tok), bf16),
            pltpu.VMEM((tok, devs * tok), f32),
            pltpu.SemaphoreType.DMA((2, devs)),
            pltpu.SemaphoreType.DMA((2, devs)),
            pltpu.SemaphoreType.DMA((2, kv_heads, devs)),
            pltpu.SemaphoreType.DMA((2, kv_heads, devs)),
        ],
        compiler_params=pltpu.CompilerParams(
            collective_id=0, has_side_effects=True, vmem_limit_bytes=48 * 1024 * 1024
        ),
        name="attention_backward",
    )(q, do, kv, seg)


def on_device(
    projected_queries,
    projected_keys,
    projected_values,
    output_gradient,
    normed_layer_input,
    segment,
    query_adapter_down,
    query_adapter_up,
    value_adapter_down,
    value_adapter_up,
):
    tok_rows = projected_queries.shape[0]
    query_width = projected_queries.shape[2]
    key_width = projected_keys.shape[2]
    key_value_heads = key_width // HEAD_SIZE
    group_devs = GROUP // tok_rows
    query_heads = query_width // HEAD_SIZE

    def by_head(x, heads):
        return x.reshape(tok_rows, 2, heads, HEAD_SIZE).transpose(1, 2, 0, 3)

    keys_values = jnp.concatenate(
        [by_head(projected_keys, key_value_heads), by_head(projected_values, key_value_heads)],
        axis=3,
    )
    query_grad, pair_grad = attention_backward(
        by_head(projected_queries, query_heads),
        by_head(output_gradient, query_heads),
        keys_values,
        segment.reshape(-1, tok_rows),
        group_devs,
    )
    grad_query = query_grad.transpose(2, 0, 1, 3).reshape(tok_rows, 2, query_width)
    grad_key = pair_grad[..., :HEAD_SIZE].transpose(2, 0, 1, 3).reshape(tok_rows, 2, key_width)
    grad_value = pair_grad[..., HEAD_SIZE:].transpose(2, 0, 1, 3).reshape(tok_rows, 2, key_width)
    adapter_input = lax.psum(
        (
            jnp.dot(normed_layer_input, query_adapter_down.T, preferred_element_type=jnp.float32),
            jnp.dot(normed_layer_input, value_adapter_down.T, preferred_element_type=jnp.float32),
        ),
        "fsdp",
    )
    query_down_part = adapter_input[0].astype(jnp.bfloat16)
    value_down_part = adapter_input[1].astype(jnp.bfloat16)
    query_flattened_rows = grad_query.reshape(tok_rows, -1)
    value_flattened_rows = grad_value.reshape(tok_rows, -1)
    adapter_rank_rows = query_adapter_up.shape[0]
    adapter_output = lax.psum(
        (
            jnp.dot(
                query_flattened_rows,
                query_adapter_up.reshape(adapter_rank_rows, -1).T,
                preferred_element_type=jnp.float32,
            ),
            jnp.dot(
                value_flattened_rows,
                value_adapter_up.reshape(adapter_rank_rows, -1).T,
                preferred_element_type=jnp.float32,
            ),
        ),
        "fsdp",
    )
    query_up_part = adapter_output[0].astype(jnp.bfloat16)
    value_up_part = adapter_output[1].astype(jnp.bfloat16)
    local_down_query = jnp.dot(
        query_up_part.T, normed_layer_input, preferred_element_type=jnp.float32
    )
    local_up_query = jnp.dot(
        query_down_part.T, query_flattened_rows, preferred_element_type=jnp.float32
    ).reshape(adapter_rank_rows, 2, -1)
    local_down_value = jnp.dot(
        value_up_part.T, normed_layer_input, preferred_element_type=jnp.float32
    )
    local_up_value = jnp.dot(
        value_down_part.T, value_flattened_rows, preferred_element_type=jnp.float32
    ).reshape(adapter_rank_rows, 2, -1)
    gradient_totals = lax.psum(
        (local_down_query, local_up_query, local_down_value, local_up_value), "ctx"
    )
    return (
        grad_query,
        grad_key,
        grad_value,
        adapter_scale * gradient_totals[0],
        adapter_scale * gradient_totals[1],
        adapter_scale * gradient_totals[2],
        adapter_scale * gradient_totals[3],
    )


def solution(mesh):
    in_specs = (
        P(("rep", "ctx"), None, "fsdp"),
        P(("rep", "ctx"), None, "fsdp"),
        P(("rep", "ctx"), None, "fsdp"),
        P(("rep", "ctx"), None, "fsdp"),
        P(("rep", "ctx"), "fsdp"),
        P("rep"),
        P(None, "fsdp"),
        P(None, None, "fsdp"),
        P(None, "fsdp"),
        P(None, None, "fsdp"),
    )
    out_specs = (
        P(("rep", "ctx"), None, "fsdp"),
        P(("rep", "ctx"), None, "fsdp"),
        P(("rep", "ctx"), None, "fsdp"),
        P("rep", "fsdp"),
        P("rep", None, "fsdp"),
        P("rep", "fsdp"),
        P("rep", None, "fsdp"),
    )
    return jax.shard_map(
        on_device, mesh=mesh, in_specs=in_specs, out_specs=out_specs, check_vma=False
    )
```

time: 459 us -> 223 us (0.49)
  waiting for transfers between devices: 184 us -> 87.9 us
  local copies, waits for them, and re-layouts: 92.1 us -> 23.1 us
  Pallas kernels: 0 us -> 46.3 us
  matrix products: 52.3 us -> 8.62 us
  other arithmetic: 41.7 us -> 3.24 us
  starting transfers between devices: 33.5 us -> 0.04 us
    ppermute x14 -> x0, waiting for transfers between devices: 95.1 us -> none  [shifted(): return lax.ppermute(x, axis, [(i, (i + by) % size) for i in range(size)])]
    pallas_call x0 -> x1, Pallas kernels: none -> 46.3 us  [attention_backward(): pl.pallas_call(functools.partial(attention_kernel, ctx, devs), out_shape=...]
    ppermute x14 -> x0, starting transfers between devices: 33.5 us -> none  [shifted(): return lax.ppermute(x, axis, [(i, (i + by) % size) for i in range(size)])]
    dot_general x10 -> x0, matrix products: 27.6 us -> none  [the longest x2 8.94 us: attend(): jnp.einsum('tgrd,lgd->tgrl', grad_part, value_rows, preferred_element_typ...]
    dynamic_slice x19 -> x0, local copies, waits for them, and re-layouts: 21.7 us -> none  [the longest x14 20.3 us: backward_step(): lax.dynamic_index_in_dim(partials, group_devs - 2 - turn_index, 0, keepdi...]
    sub x2 -> x0, matrix products: 14.6 us -> none  [attend(): weights = jnp.exp(scores - highest)]
    convert_element_type x3 -> x0, other arithmetic: 14 us -> none  [the longest x2 13 us: attend(): rounded = weights.astype(jnp.bfloat16)]
    add x9 -> x0, other arithmetic: 13.4 us -> none  [the longest x7 13.2 us: backward_step(): carried + lax.dynamic_index_in_dim(partials, group_devs - 2 - turn_index,...]
  transfers between devices with their start and end apart: 15 -> 1, of which waited for: 15 -> 1; matrix products, arithmetic and copies ran while one was open for 6% -> 3% of each run, Pallas kernels for 0% -> 0%
where the time goes in v1:
time: 223 us
  waiting for transfers between devices  87.9 us (39%)
  Pallas kernels  46.3 us (21%)
  blocking collectives  39.3 us (18%)
  local copies, waits for them, and re-layouts  23.1 us (10%)
  between operations  14.2 us (6%)
  matrix products  8.62 us (4%)
  other arithmetic  3.24 us (1%)
    psum x1, waiting for transfers between devices, on_device(): lax.psum((local_down_query, local_up_query, local_down_value, local_up_va...  87.8 us
    pallas_call x1, Pallas kernels, attention_backward(): pl.pallas_call(functools.partial(attention_kernel, ctx, devs), out_shape=...  46.3 us
    psum x1, blocking collectives, on_device(): lax.psum((local_down_query, local_up_query, local_down_value, local_up_va...  39.3 us
    unnamed x23, local copies, waits for them, and re-layouts  17 us
  transfers between devices with their start and end apart: 1, of which 1 were waited for; matrix products, arithmetic and copies ran while one was open for 3% of the time, Pallas kernels for 0%

profile of v1, /device:TPU:0, one launch (start us, length us, event | category | flops | bytes accessed | tf_op | source)
XLA Modules:
  0.0 222.7 jit_solution(9065150531625814492)
XLA Ops:
  7.2 3.8 %copy.19 = bf16[128,2,2048]{0,2,1:T(8,128)(2,1)} copy(bf16[128,2,2048]{2,1,0:T(2,128)(2,1)} %param.10) | data formatting | bytes 2097152 | tf_op args[0]
  11.0 1.6 copy.20
  12.7 3.7 %copy.21 = bf16[128,2,2048]{0,2,1:T(8,128)(2,1)} copy(bf16[128,2,2048]{2,1,0:T(2,128)(2,1)} %param.13) | data formatting | bytes 2097152 | tf_op args[3]
  16.4 2.3 %copy.22 = bf16[128,2,16,128]{3,0,2,1:T(8,128)(2,1)} copy(bf16[128,2,16,128]{0,3,2,1:T(8,128)(2,1)} %bitcast.59) | data formatting | bytes 2097152 | tf_op jit(solution)/shard_map/reshape | solution.py:310
  18.7 0.1 copy.23
  18.9 1.0 copy.25
  20.2 1.2 copy-done.1
  21.4 46.3 %attention_backward.1 = (bf16[2,16,128,128]{3,2,1,0:T(8,128)(2,1)S(1)}, bf16[2,2,128,256]{3,2,1,0:T(8,128)(2,1)S(1)}) custom-call(bf16[2,16,128,128]{3,2,1,0:T(8,128)(2,1)S(1)} %bitcast.51, bf16[2,16,128,128]{3,2,1,0:T(8,128)(2,1)S(1)} %bitcast.52, bf16[2,2,128,256]{3,2,1,0:T(8,128)(2,1)S(1)} %pad_maximum_fusion.kv_ref, s32[32,128]{1,0:T(8,128)S(1)} %bitcast.54), custom_call_target="tpu_custom_call" | custom-call | tf_op jit(solution)/shard_map/attention_backward/pallas_call | solution.py:262
  67.7 1.0 copy-done.2
  68.9 1.6 copy.27
  70.5 0.9 copy.37
  71.5 1.5 fusion.1
  73.0 2.2 fusion
  75.1 3.2 %fusion.4 = f32[16,2,2048]{2,0,1:T(8,128)} fusion(bf16[2,2048,128]{2,1,0:T(8,128)(2,1)S(1)} %bitcast.56, bf16[128,8192]{1,0:T(8,128)(2,1)S(1)} %copy-done, bf16[16,8192]{1,0:T(8,128)(2,1)} %param.16), kind=kOutput, calls=%fused_computation.8 | convolution fusion | flops 50333696 | bytes 3670016 | tf_op jit(solution)/shard_map/dot_general | solution.py:358
  78.4 0.8 copy.34
  79.2 1.8 fusion.5
  80.9 39.3 %psum.31 = f32[16,2,256]{2,0,1:T(8,128)S(1)} all-reduce(f32[16,2,256]{2,0,1:T(8,128)S(1)} %fusion.5), channel_id=1, replica_groups=mesh['rep'=1,'ctx'=32,'fsdp'=1] {'ctx'}, use_global_device_ids=true, to_apply=%region_3.0 | all-reduce | flops 8192 | bytes 65536 | tf_op jit(solution)/shard_map/psum | solution.py:367
  120.3 0.6 copy.36
  120.9 2.0 copy.32
  123.1 0.8 copy.33
  123.9 87.8 %all-reduce.3.cloned.1.call-done = (f32[16,8192]{1,0:T(8,128)}, f32[16,2,2048]{2,0,1:T(8,128)}, f32[16,8192]{1,0:T(8,128)}) async-done(((f32[16,8192]{1,0:T(8,128)}, f32[16,2,2048]{2,0,1:T(8,128)}, f32[16,8192]{1,0:T(8,128)}), (f32[16,8192]{1,0:T(8,128)}, f32[16,2,2048]{2,0,1:T(8,128)}, f32[16,8192]{1,0:T(8,128)})) %all-reduce.3.cloned.1.call-update) | async-done | bytes 1310736 | tf_op jit(solution)/shard_map/psum | solution.py:367
  211.7 1.0 broadcast_multiply_fusion.2
  212.7 0.9 copy.35
  213.6 2.2 %broadcast_multiply_fusion = (f32[16,8192]{1,0:T(8,128)}, f32[16,8192]{1,0:T(8,128)}) fusion(f32[16,8192]{1,0:T(8,128)} %get-tuple-element.27, f32[16,8192]{1,0:T(8,128)} %get-tuple-element.25), kind=kLoop, calls=%fused_computation.11 | loop fusion | flops 262144 | bytes 2097152 | tf_op jit(solution)/shard_map/mul | solution.py:376
  (20 shorter events, 0.7 us)
Async XLA Ops:
  7.2 64.3 %copy-start = (bf16[128,8192]{1,0:T(8,128)(2,1)S(1)}, bf16[128,8192]{1,0:T(8,128)(2,1)}, u32[]{:S(2)}) copy-start(bf16[128,8192]{1,0:T(8,128)(2,1)} %param.14) | copy-start | bytes 6291460
  7.2 204.5 %all-reduce.3.cloned.1.call-start = ((), (), s32[]{:S(2)}) async-start(), calls=%async_computation | async-start | bytes 2621440 | tf_op jit(solution)/shard_map/psum | solution.py:367
  12.7 6.0 %copy-start.4 = (bf16[128,2,256]{2,1,0:T(2,128)(2,1)S(1)}, bf16[128,2,256]{2,1,0:T(2,128)(2,1)}, u32[]{:S(2)}) copy-start(bf16[128,2,256]{2,1,0:T(2,128)(2,1)} %param.11) | copy-start | bytes 393220
  16.4 3.8 %copy-start.3 = (s32[4096]{0:T(1024)S(1)}, s32[4096]{0:T(1024)}, u32[]{:S(2)}) copy-start(s32[4096]{0:T(1024)} %param.15) | copy-start | bytes 49156
  20.1 48.8 %copy-start.5 = (bf16[16,2,256]{2,1,0:T(2,128)(2,1)S(1)}, bf16[16,2,256]{2,1,0:T(2,128)(2,1)}, u32[]{:S(2)}) copy-start(bf16[16,2,256]{2,1,0:T(2,128)(2,1)} %param.19) | copy-start | bytes 49156
  20.2 1.2 copy-start.1
  67.7 1.0 copy-start.2
Sparse Core Ops, SparseCore 0:
  78.5 133.1 all-reduce.2

commit v2 on v1

--- a/solution.py
+++ b/solution.py
@@ -23,12 +23,21 @@
 def attention_kernel(
     ctx,
     devs,
+    with_adapters,
     q_ref,
     do_ref,
     kv_ref,
     seg_ref,
-    dq_ref,
-    gkv_ref,
+    *refs,
+):
+    if with_adapters:
+        x_ref, down_ref, q_up_ref, v_up_ref = refs[:4]
+        dq_ref, gkv_ref, qd_out, qu_out, vd_out, vu_out = refs[4:10]
+        refs = refs[10:]
+    else:
+        dq_ref, gkv_ref = refs[:2]
+        refs = refs[2:]
+    (
     kv_buf,
     part_send,
     part_recv,
@@ -40,7 +49,10 @@
     g_recv,
     r_send,
     r_recv,
-):
+    ) = refs[:11]
+    if with_adapters:
+        downs, q_act, *rest = refs[11:]
+        q_bufs, v_bufs = rest[:10], rest[10:]
     kv_heads = kv_ref.shape[1]
     tok = kv_ref.shape[2]
     repeat = q_ref.shape[1] // kv_heads
@@ -63,7 +75,17 @@
     for d in range(1, devs):
         pl.semaphore_signal(barrier, inc=1, device_id={"ctx": ahead(d)}, device_id_type=MESH)
         pl.semaphore_signal(barrier, inc=1, device_id={"ctx": behind(d)}, device_id_type=MESH)
-    pl.semaphore_wait(barrier, 2 * (devs - 1))
+    planes = ctx // devs
+    plane = me // devs
+    far = range(1, planes) if with_adapters else range(0)
+    for j in far:
+        pl.semaphore_signal(
+            barrier,
+            inc=1,
+            device_id={"ctx": lax.rem(me + j * devs, ctx)},
+            device_id_type=MESH,
+        )
+    pl.semaphore_wait(barrier, 2 * (devs - 1) + len(far))
 
     def gather_copy(h, d):
         return pltpu.make_async_remote_copy(
@@ -126,6 +148,101 @@
         if d == 0:
             block = jnp.where(columns <= rows, block, MASKED)
         bias[:, d * tok : (d + 1) * tok] = block
+
+    def within(j):
+        return lax.rem(p0 + j, devs)
+
+    def scatter_copy(bufs, j):
+        part, landed, s_send, s_recv = bufs[0], bufs[1], bufs[4], bufs[5]
+        return pltpu.make_async_remote_copy(
+            src_ref=part.at[within(j)],
+            dst_ref=landed.at[j],
+            send_sem=s_send.at[j],
+            recv_sem=s_recv.at[j],
+            device_id={"ctx": plane * devs + within(j)},
+            device_id_type=MESH,
+        )
+
+    def plane_copy(bufs, j):
+        across, s_send, s_recv = bufs[2], bufs[6], bufs[7]
+        return pltpu.make_async_remote_copy(
+            src_ref=across.at[plane],
+            dst_ref=across.at[plane],
+            send_sem=s_send.at[j],
+            recv_sem=s_recv.at[j],
+            device_id={"ctx": lax.rem(me + j * devs, ctx)},
+            device_id_type=MESH,
+        )
+
+    def spread_copy(bufs, j):
+        whole, s_send, s_recv = bufs[3], bufs[8], bufs[9]
+        return pltpu.make_async_remote_copy(
+            src_ref=whole.at[p0],
+            dst_ref=whole.at[p0],
+            send_sem=s_send.at[j],
+            recv_sem=s_recv.at[j],
+            device_id={"ctx": plane * devs + within(j)},
+            device_id_type=MESH,
+        )
+
+    def start_scatter(bufs):
+        for j in range(1, devs):
+            scatter_copy(bufs, j).start()
+
+    def start_planes(bufs):
+        total = bufs[0][p0].astype(jnp.float32)
+        for j in range(1, devs):
+            scatter_copy(bufs, j).wait_recv()
+            total = total + bufs[1][j].astype(jnp.float32)
+        bufs[2][plane] = total.astype(jnp.bfloat16)
+        for j in range(1, planes):
+            plane_copy(bufs, j).start()
+
+    def start_spread(bufs):
+        for j in range(1, planes):
+            plane_copy(bufs, j).wait_recv()
+        total = bufs[2][0].astype(jnp.float32)
+        for j in range(1, planes):
+            total = total + bufs[2][j].astype(jnp.float32)
+        bufs[3][p0] = total.astype(jnp.bfloat16)
+        for j in range(1, devs):
+            spread_copy(bufs, j).start()
+
+    def finish(bufs, down_out, up_out, up_pieces):
+        for j in range(1, devs):
+            spread_copy(bufs, j).wait_recv()
+        width = down_out.shape[1] // devs
+        up_width = up_out.shape[1] // up_pieces
+        for p in range(devs):
+            down_out[:, p * width : (p + 1) * width] = adapter_scale * bufs[3][
+                p, :, :width
+            ].astype(jnp.float32)
+            if p < up_pieces:
+                up_out[:, p * up_width : (p + 1) * up_width] = adapter_scale * bufs[3][
+                    p, :, width:
+                ].astype(jnp.float32)
+        for j in range(1, devs):
+            scatter_copy(bufs, j).wait_send()
+            spread_copy(bufs, j).wait_send()
+        for j in range(1, planes):
+            plane_copy(bufs, j).wait_send()
+
+    def project_down(bufs, act):
+        width = x_ref.shape[1] // devs
+        for p in range(devs):
+            bufs[0][p, :, :width] = jnp.dot(
+                act, x_ref[:, p * width : (p + 1) * width], preferred_element_type=jnp.float32
+            ).astype(jnp.bfloat16)
+
+    if with_adapters:
+        acts = lax.dot_general(
+            down_ref[...], x_ref[...], (((1,), (1,)), ((), ())), preferred_element_type=jnp.float32
+        ).astype(jnp.bfloat16)
+        downs[...] = acts
+        q_act[...] = jnp.zeros_like(q_act)
+        rank = q_act.shape[0]
+        for p in range(2 * kv_heads, devs):
+            v_bufs[0][p, :, x_ref.shape[1] // devs :] = jnp.zeros((rank, HEAD_SIZE), jnp.bfloat16)
 
     def attend(h, slots, limit):
         keys = slots * tok
@@ -159,6 +276,25 @@
                 return inner
 
             lax.fori_loop(0, repeat, one_head, 0, unroll=2)
+            if with_adapters:
+                dq_all = jnp.concatenate(
+                    [dq_ref[h, g * repeat + r] for r in range(repeat)], axis=1
+                )
+                q_act[...] += lax.dot_general(
+                    q_up_ref[h, g],
+                    dq_all,
+                    (((1,), (1,)), ((), ())),
+                    preferred_element_type=jnp.float32,
+                )
+                up = jnp.dot(downs[:rank], dq_all, preferred_element_type=jnp.float32)
+                up = up.astype(jnp.bfloat16)
+                width = x_ref.shape[1] // devs
+                each = repeat * HEAD_SIZE * 2 * kv_heads // devs
+                pieces = repeat * HEAD_SIZE // each
+                for i in range(pieces):
+                    q_bufs[0][(h * kv_heads + g) * pieces + i, :, width:] = up[
+                        :, i * each : (i + 1) * each
+                    ]
             q_all = q_ref[h, pl.ds(g * repeat, repeat)].reshape(repeat * tok, HEAD_SIZE)
             do_all = do_ref[h, pl.ds(g * repeat, repeat)].reshape(repeat * tok, HEAD_SIZE)
             dk = lax.dot_general(
@@ -208,6 +344,10 @@
 
     attend(big, devs, ps + mid + 1)
 
+    if with_adapters:
+        project_down(q_bufs, q_act[...].astype(jnp.bfloat16))
+        start_scatter(q_bufs)
+
     for d in range(1, devs):
         for g in range(kv_heads):
 
@@ -228,6 +368,29 @@
 
     gkv_ref[...] = own_part[...].astype(jnp.bfloat16)
 
+    if with_adapters:
+        v_act = jnp.zeros(q_act.shape, jnp.float32)
+        for h in range(2):
+            for g in range(kv_heads):
+                gv = gkv_ref[h, g, :, HEAD_SIZE:]
+                v_act = v_act + lax.dot_general(
+                    v_up_ref[h, g],
+                    gv,
+                    (((1,), (1,)), ((), ())),
+                    preferred_element_type=jnp.float32,
+                )
+                v_bufs[0][h * kv_heads + g, :, x_ref.shape[1] // devs :] = jnp.dot(
+                    downs[rank:], gv, preferred_element_type=jnp.float32
+                ).astype(jnp.bfloat16)
+        project_down(v_bufs, v_act.astype(jnp.bfloat16))
+        start_scatter(v_bufs)
+        start_planes(q_bufs)
+        start_planes(v_bufs)
+        start_spread(q_bufs)
+        start_spread(v_bufs)
+        finish(q_bufs, qd_out, qu_out, devs)
+        finish(v_bufs, vd_out, vu_out, 2 * kv_heads)
+
     for d in range(1, devs):
 
         @pl.when(ps + d < devs)
@@ -251,40 +414,57 @@
                 return_copy(small, g, d).wait_send()
 
 
-def attention_backward(q, do, kv, seg, devs):
+def attention_backward(q, do, kv, seg, devs, adapters=None):
     heads, tok = q.shape[1], q.shape[2]
     kv_heads = kv.shape[1]
     repeat = heads // kv_heads
     ctx = lax.axis_size("ctx")
+    planes = ctx // devs
     bf16, f32 = jnp.bfloat16, jnp.float32
     pair = 2 * HEAD_SIZE
     vmem = pl.BlockSpec(memory_space=pltpu.VMEM)
+    operands = (q, do, kv, seg)
+    results = [jax.ShapeDtypeStruct(q.shape, bf16), jax.ShapeDtypeStruct(kv.shape, bf16)]
+    scratch = [
+        pltpu.VMEM((2, devs, kv_heads, tok, pair), bf16),
+        pltpu.VMEM((2, kv_heads, devs, tok, pair), bf16),
+        pltpu.VMEM((2, kv_heads, devs, tok, pair), bf16),
+        pltpu.VMEM((2, kv_heads, tok, pair), f32),
+        pltpu.VMEM((repeat * tok, devs * tok), bf16),
+        pltpu.VMEM((repeat * tok, devs * tok), bf16),
+        pltpu.VMEM((tok, devs * tok), f32),
+        pltpu.SemaphoreType.DMA((2, devs)),
+        pltpu.SemaphoreType.DMA((2, devs)),
+        pltpu.SemaphoreType.DMA((2, kv_heads, devs)),
+        pltpu.SemaphoreType.DMA((2, kv_heads, devs)),
+    ]
+    if adapters is not None:
+        operands = operands + adapters
+        rank = adapters[1].shape[0] // 2
+        width = adapters[0].shape[1]
+        q_width, v_width = 2 * heads * HEAD_SIZE, 2 * kv_heads * HEAD_SIZE
+        results += [
+            jax.ShapeDtypeStruct((rank, n), f32) for n in (width, q_width, width, v_width)
+        ]
+        scratch += [pltpu.VMEM((2 * rank, tok), bf16), pltpu.VMEM((rank, tok), f32)]
+        for columns in ((width + q_width) // devs, width // devs + HEAD_SIZE):
+            scratch += [
+                pltpu.VMEM((n, rank, columns), bf16) for n in (devs, devs, planes, devs)
+            ]
+            scratch += [
+                pltpu.SemaphoreType.DMA((n,)) for n in (devs, devs, planes, planes, devs, devs)
+            ]
     return pl.pallas_call(
-        functools.partial(attention_kernel, ctx, devs),
-        out_shape=(
-            jax.ShapeDtypeStruct(q.shape, bf16),
-            jax.ShapeDtypeStruct(kv.shape, bf16),
-        ),
-        in_specs=[vmem] * 4,
-        out_specs=(vmem, vmem),
-        scratch_shapes=[
-            pltpu.VMEM((2, devs, kv_heads, tok, pair), bf16),
-            pltpu.VMEM((2, kv_heads, devs, tok, pair), bf16),
-            pltpu.VMEM((2, kv_heads, devs, tok, pair), bf16),
-            pltpu.VMEM((2, kv_heads, tok, pair), f32),
-            pltpu.VMEM((repeat * tok, devs * tok), bf16),
-            pltpu.VMEM((repeat * tok, devs * tok), bf16),
-            pltpu.VMEM((tok, devs * tok), f32),
-            pltpu.SemaphoreType.DMA((2, devs)),
-            pltpu.SemaphoreType.DMA((2, devs)),
-            pltpu.SemaphoreType.DMA((2, kv_heads, devs)),
-            pltpu.SemaphoreType.DMA((2, kv_heads, devs)),
-        ],
+        functools.partial(attention_kernel, ctx, devs, adapters is not None),
+        out_shape=tuple(results),
+        in_specs=[vmem] * len(operands),
+        out_specs=(vmem,) * len(results),
+        scratch_shapes=scratch,
         compiler_params=pltpu.CompilerParams(
-            collective_id=0, has_side_effects=True, vmem_limit_bytes=48 * 1024 * 1024
+            collective_id=0, has_side_effects=True, vmem_limit_bytes=52 * 1024 * 1024
         ),
         name="attention_backward",
-    )(q, do, kv, seg)
+    )(*operands)
 
 
 def on_device(
@@ -313,16 +493,37 @@
         [by_head(projected_keys, key_value_heads), by_head(projected_values, key_value_heads)],
         axis=3,
     )
-    query_grad, pair_grad = attention_backward(
+    whole_width = lax.axis_size("fsdp") == 1 and 2 * key_value_heads <= group_devs
+    adapters = None
+    if whole_width:
+        rank = query_adapter_up.shape[0]
+        adapters = (
+            normed_layer_input,
+            jnp.concatenate([query_adapter_down, value_adapter_down], axis=0),
+            query_adapter_up.reshape(rank, 2, key_value_heads, -1).transpose(1, 2, 0, 3),
+            value_adapter_up.reshape(rank, 2, key_value_heads, -1).transpose(1, 2, 0, 3),
+        )
+    query_grad, pair_grad, *totals = attention_backward(
         by_head(projected_queries, query_heads),
         by_head(output_gradient, query_heads),
         keys_values,
         segment.reshape(-1, tok_rows),
         group_devs,
+        adapters,
     )
     grad_query = query_grad.transpose(2, 0, 1, 3).reshape(tok_rows, 2, query_width)
     grad_key = pair_grad[..., :HEAD_SIZE].transpose(2, 0, 1, 3).reshape(tok_rows, 2, key_width)
     grad_value = pair_grad[..., HEAD_SIZE:].transpose(2, 0, 1, 3).reshape(tok_rows, 2, key_width)
+    if whole_width:
+        return (
+            grad_query,
+            grad_key,
+            grad_value,
+            totals[0],
+            totals[1].reshape(rank, 2, query_width),
+            totals[2],
+            totals[3].reshape(rank, 2, key_width),
+        )
     adapter_input = lax.psum(
         (
             jnp.dot(normed_layer_input, query_adapter_down.T, preferred_element_type=jnp.float32),

time: 223 us -> 88.1 us (0.40)
  waiting for transfers between devices: 87.9 us -> 0 us
  blocking collectives: 39.3 us -> 0 us
  Pallas kernels: 46.3 us -> 68.5 us
  between operations: 14.2 us -> 0.78 us
  matrix products: 8.62 us -> 0 us
  local copies, waits for them, and re-layouts: 23.1 us -> 17.6 us
  other arithmetic: 3.24 us -> 0.86 us
    psum x1 -> x0, waiting for transfers between devices: 87.8 us -> none  [on_device(): lax.psum((local_down_query, local_up_query, local_down_value, local_up_va...]
    psum x1 -> x0, blocking collectives: 39.3 us -> none  [on_device(): lax.psum((local_down_query, local_up_query, local_down_value, local_up_va...]
    pallas_call x1, Pallas kernels: 46.3 us -> 68.5 us  [attention_backward(): pl.pallas_call(functools.partial(attention_kernel, ctx, devs, adapters is...]
    dot_general x4 -> x0, matrix products: 8.62 us -> none  [the longest x1 3.2 us: on_device(): jnp.dot(query_down_part.T, query_flattened_rows, preferred_element_type=j...]
    unnamed x23 -> x19, local copies, waits for them, and re-layouts: 17 us -> 9.34 us
    reshape x0 -> x6, local copies, waits for them, and re-layouts: none -> 3.46 us  [the longest x2 1.04 us: on_device(): query_adapter_up.reshape(rank, 2, key_value_heads, -1).transpose(1, 2, 0, 3)]
    mul x3 -> x0, other arithmetic: 3.21 us -> none  [the longest x1 2.23 us: on_device(): adapter_scale * gradient_totals[2]]
  transfers between devices with their start and end apart: 1 -> 0, of which waited for: 1 -> 0; matrix products, arithmetic and copies ran while one was open for 3% -> 0% of each run, Pallas kernels for 0% -> 0%
where the time goes in v2:
time: 88.1 us; the launch traced here: 87.8 us
  Pallas kernels  68.5 us (78%)
  local copies, waits for them, and re-layouts  17.6 us (20%)
    pallas_call x1, Pallas kernels, attention_backward(): pl.pallas_call(functools.partial(attention_kernel, ctx, devs, adapters is...  68.5 us
    unnamed x19, local copies, waits for them, and re-layouts  9.34 us
    reshape x4, local copies, waits for them, and re-layouts, by_head(): return x.reshape(tok_rows, 2, heads, HEAD_SIZE).transpose(1, 2, 0, 3)  2.9 us

profile of v2, /device:TPU:0, one launch (start us, length us, event | category | flops | bytes accessed | tf_op | source)
XLA Modules:
  0.0 87.8 jit_solution(14032426640934075446)
XLA Ops:
  0.7 0.8 reshape.63
  1.5 1.0 %copy.21 = bf16[128,2,256]{0,2,1:T(8,128)(2,1)S(1)} copy(bf16[128,2,256]{2,1,0:T(2,128)(2,1)} %param.11) | data formatting | bytes 262144 | tf_op args[1]
  2.6 0.1 copy.22
  2.7 1.0 %copy.23 = bf16[128,2,256]{0,2,1:T(8,128)(2,1)S(1)} copy(bf16[128,2,256]{2,1,0:T(2,128)(2,1)} %param.12) | data formatting | bytes 262144 | tf_op args[2]
  3.7 0.1 copy.24
  3.9 1.0 %reshape.62 = bf16[16,2,2,1024]{3,2,1,0:T(2,128)(2,1)S(1)} reshape(bf16[16,2,2048]{2,1,0:T(2,128)(2,1)} %param.17) | data formatting | bytes 262144 | tf_op jit(solution)/shard_map/reshape | solution.py:503
  5.0 0.0 copy-done.3
  5.0 0.8 pad_maximum_fusion.refs_1_
  5.8 1.0 %copy.17 = bf16[128,2,2048]{0,2,1:T(8,128)(2,1)S(1)} copy(bf16[128,2,2048]{2,1,0:T(2,128)(2,1)S(1)} %copy-done.1) | data formatting | bytes 2097152 | tf_op args[0]
  6.9 0.0 copy-start.2
  6.9 1.3 %copy.18 = bf16[128,2,16,128]{3,0,2,1:T(8,128)(2,1)} copy(bf16[128,2,16,128]{0,3,2,1:T(8,128)(2,1)S(1)} %bitcast.29) | data formatting | bytes 2097152 | tf_op jit(solution)/shard_map/reshape | solution.py:490
  8.2 1.0 %copy.19 = bf16[128,2,2048]{0,2,1:T(8,128)(2,1)S(1)} copy(bf16[128,2,2048]{2,1,0:T(2,128)(2,1)S(1)} %copy-done.2) | data formatting | bytes 2097152 | tf_op args[3]
  9.2 1.3 %copy.20 = bf16[128,2,16,128]{3,0,2,1:T(8,128)(2,1)} copy(bf16[128,2,16,128]{0,3,2,1:T(8,128)(2,1)S(1)} %bitcast.30) | data formatting | bytes 2097152 | tf_op jit(solution)/shard_map/reshape | solution.py:490
  10.6 68.5 %attention_backward.1 = (bf16[2,16,128,128]{3,2,1,0:T(8,128)(2,1)}, bf16[2,2,128,256]{3,2,1,0:T(8,128)(2,1)S(1)}, f32[16,8192]{1,0:T(8,128)S(1)}, f32[16,4096]{1...) custom-call(bf16[2,16,128,128]{3,2,1,0:T(8,128)(2,1)} %bitcast.26, bf16[2,16,128,128]{3,2,1,0:T(8,128)(2,1)} %bitcast.27, ...), custom_call_target="tpu_custom_call" | custom-call | tf_op jit(solution)/shard_map/attention_backward/pallas_call | solution.py:457
  79.1 1.6 %copy.29 = bf16[128,2,16,128]{0,3,2,1:T(8,128)(2,1)S(1)} copy(bf16[128,2,16,128]{3,0,2,1:T(8,128)(2,1)} %bitcast.31) | data formatting | bytes 2097152 | tf_op jit(solution)/shard_map/transpose | solution.py:514
  80.7 2.0 %copy.32 = bf16[128,2,2048]{2,1,0:T(2,128)(2,1)} copy(bf16[128,2,2048]{0,2,1:T(8,128)(2,1)S(1)} %bitcast.28) | data formatting | bytes 2097152
  82.7 0.6 reshape.61
  83.4 0.9 %reshape.60 = f32[16,2,2048]{2,1,0:T(2,128)} reshape(f32[16,4096]{1,0:T(8,128)S(1)} %get-tuple-element.16) | data formatting | bytes 524288 | tf_op jit(solution)/shard_map/reshape | solution.py:523
  84.4 0.1 copy.31
  84.5 0.8 copy.34
  85.3 0.1 copy.30
  85.4 0.8 copy.33
  86.2 0.8 copy.45
  87.0 0.8 copy.46
  (12 shorter events, 0.1 us)
Async XLA Ops:
  0.6 4.3 %copy-start.3 = (bf16[16,8192]{1,0:T(8,128)(2,1)S(1)}, bf16[16,8192]{1,0:T(8,128)(2,1)}, u32[]{:S(2)}) copy-start(bf16[16,8192]{1,0:T(8,128)(2,1)} %param.18) | copy-start | bytes 786436
  0.6 4.3 %copy-start.4 = (bf16[16,8192]{1,0:T(8,128)(2,1)S(1)}, bf16[16,8192]{1,0:T(8,128)(2,1)}, u32[]{:S(2)}) copy-start(bf16[16,8192]{1,0:T(8,128)(2,1)} %param.16) | copy-start | bytes 786436
  0.7 5.2 %copy-start.1 = (bf16[128,2,2048]{2,1,0:T(2,128)(2,1)S(1)}, bf16[128,2,2048]{2,1,0:T(2,128)(2,1)}, u32[]{:S(2)}) copy-start(bf16[128,2,2048]{2,1,0:T(2,128)(2,1)} %param.10) | copy-start | bytes 3145732
  6.9 1.3 %copy-start.2 = (bf16[128,2,2048]{2,1,0:T(2,128)(2,1)S(1)}, bf16[128,2,2048]{2,1,0:T(2,128)(2,1)}, u32[]{:S(2)}) copy-start(bf16[128,2,2048]{2,1,0:T(2,128)(2,1)} %param.13) | copy-start | bytes 3145732
  8.2 2.4 %copy-start = (s32[4096]{0:T(1024)S(1)}, s32[4096]{0:T(1024)}, u32[]{:S(2)}) copy-start(s32[4096]{0:T(1024)} %param.15) | copy-start | bytes 49156

commit v3 on v2

v3 whole, which is shorter than its diff:
```python
import functools
import math

import jax
import jax.numpy as jnp
from jax import lax
from jax.experimental import pallas as pl
from jax.experimental.pallas import tpu as pltpu
from jax.sharding import PartitionSpec as P

MESH = pl.DeviceIdType.MESH
MASKED = -1e30

QUERY_HEADS = 32
KEY_VALUE_HEADS = 4
HEAD_SIZE = 128
GROUP = 1024


adapter_scale = 2.0


def attention_kernel(
    ctx,
    devs,
    with_adapters,
    q_ref,
    do_ref,
    k_ref,
    v_ref,
    seg_ref,
    *refs,
):
    if with_adapters:
        x_ref, q_down_ref, v_down_ref, q_up_ref, v_up_ref = refs[:5]
        dq_ref, gk_ref, gv_ref, qd_out, qu_out, vd_out, vu_out = refs[5:12]
        refs = refs[12:]
    else:
        dq_ref, gk_ref, gv_ref = refs[:3]
        refs = refs[3:]
    kv_buf, part_send, part_recv, own_part, p_scr, w_scr, bias, g_send, g_recv, r_send, r_recv = (
        refs[:11]
    )
    if with_adapters:
        q_down, v_down, q_up, v_up, q_act = refs[11:16]
        q_bufs, v_bufs = refs[16:26], refs[26:]
    tok = k_ref.shape[1]
    kv_heads = k_ref.shape[2] // HEAD_SIZE
    repeat = q_ref.shape[2] // k_ref.shape[2]
    group_width = repeat * HEAD_SIZE
    mid = devs // 2
    scaling = HEAD_SIZE ** (-0.5)
    exponent = scaling * math.log2(math.e)
    me = lax.axis_index("ctx")
    p0 = lax.rem(me, devs)
    small = p0 // mid
    big = 1 - small
    ps = lax.rem(p0, mid)

    def ahead(d):
        return lax.rem(me + d, ctx)

    def behind(d):
        return lax.rem(me + ctx - d, ctx)

    for h in range(2):
        for g in range(kv_heads):
            lanes = slice(g * HEAD_SIZE, (g + 1) * HEAD_SIZE)
            kv_buf[h, 0, g, :, :HEAD_SIZE] = k_ref[h, :, lanes]
            kv_buf[h, 0, g, :, HEAD_SIZE:] = v_ref[h, :, lanes]

    barrier = pltpu.get_barrier_semaphore()
    for d in range(1, devs):
        pl.semaphore_signal(barrier, inc=1, device_id={"ctx": ahead(d)}, device_id_type=MESH)
        pl.semaphore_signal(barrier, inc=1, device_id={"ctx": behind(d)}, device_id_type=MESH)
    planes = ctx // devs
    plane = me // devs
    far = range(1, planes) if with_adapters else range(0)
    for j in far:
        pl.semaphore_signal(
            barrier,
            inc=1,
            device_id={"ctx": lax.rem(me + j * devs, ctx)},
            device_id_type=MESH,
        )
    pl.semaphore_wait(barrier, 2 * (devs - 1) + len(far))

    def gather_copy(h, d):
        return pltpu.make_async_remote_copy(
            src_ref=kv_buf.at[h, 0],
            dst_ref=kv_buf.at[h, d],
            send_sem=g_send.at[h, d],
            recv_sem=g_recv.at[h, d],
            device_id={"ctx": ahead(d)},
            device_id_type=MESH,
        )

    def return_copy(which, h, g, d):
        return pltpu.make_async_remote_copy(
            src_ref=part_send.at[which, h, g, d],
            dst_ref=part_recv.at[which, h, g, d],
            send_sem=r_send.at[which, h, g, d],
            recv_sem=r_recv.at[which, h, g, d],
            device_id={"ctx": behind(d)},
            device_id_type=MESH,
        )

    for d in range(1, mid):

        @pl.when(ps + d < mid)
        def _():
            gather_copy(small, d).start()

    for d in range(1, devs):

        @pl.when((ps + d >= mid) & (ps + d < devs))
        def _():
            gather_copy(small, d).start()

    for d in range(1, mid):

        @pl.when(ps + d < mid)
        def _():
            gather_copy(big, d).start()

    for d in range(1, mid):

        @pl.when(d > ps)
        def _():
            kv_buf[small, d] = jnp.zeros(kv_buf.shape[2:], kv_buf.dtype)

        @pl.when(d > ps)
        def _():
            kv_buf[big, mid + d] = jnp.zeros(kv_buf.shape[2:], kv_buf.dtype)

    own_ids = jnp.transpose(
        jnp.broadcast_to(seg_ref[pl.ds(me, 1), :].astype(jnp.float32), (tok, tok))
    )
    rows = lax.broadcasted_iota(jnp.int32, (tok, tok), 0)
    columns = lax.broadcasted_iota(jnp.int32, (tok, tok), 1)
    for d in range(devs):
        ids = seg_ref[pl.ds(behind(d), 1), :].astype(jnp.float32)
        block = jnp.where(own_ids == ids, 0.0, MASKED)
        if d == 0:
            block = jnp.where(columns <= rows, block, MASKED)
        bias[1, :, d * tok : (d + 1) * tok] = jnp.where(d <= ps + mid, block, MASKED)
        if d < mid:
            bias[0, :, d * tok : (d + 1) * tok] = jnp.where(d <= ps, block, MASKED)

    def within(j):
        return lax.rem(p0 + j, devs)

    def scatter_copy(bufs, j):
        part, landed, s_send, s_recv = bufs[0], bufs[1], bufs[4], bufs[5]
        return pltpu.make_async_remote_copy(
            src_ref=part.at[within(j)],
            dst_ref=landed.at[j],
            send_sem=s_send.at[j],
            recv_sem=s_recv.at[j],
            device_id={"ctx": plane * devs + within(j)},
            device_id_type=MESH,
        )

    def plane_copy(bufs, j):
        across, s_send, s_recv = bufs[2], bufs[6], bufs[7]
        return pltpu.make_async_remote_copy(
            src_ref=across.at[plane],
            dst_ref=across.at[plane],
            send_sem=s_send.at[j],
            recv_sem=s_recv.at[j],
            device_id={"ctx": lax.rem(me + j * devs, ctx)},
            device_id_type=MESH,
        )

    def spread_copy(bufs, j):
        whole, s_send, s_recv = bufs[3], bufs[8], bufs[9]
        return pltpu.make_async_remote_copy(
            src_ref=whole.at[p0],
            dst_ref=whole.at[p0],
            send_sem=s_send.at[j],
            recv_sem=s_recv.at[j],
            device_id={"ctx": plane * devs + within(j)},
            device_id_type=MESH,
        )

    def start_scatter(bufs):
        for j in range(1, devs):
            scatter_copy(bufs, j).start()

    def start_planes(bufs):
        total = bufs[0][p0].astype(jnp.float32)
        for j in range(1, devs):
            scatter_copy(bufs, j).wait_recv()
            total = total + bufs[1][j].astype(jnp.float32)
        bufs[2][plane] = total.astype(jnp.bfloat16)
        for j in range(1, planes):
            plane_copy(bufs, j).start()

    def start_spread(bufs):
        for j in range(1, planes):
            plane_copy(bufs, j).wait_recv()
        total = bufs[2][0].astype(jnp.float32)
        for j in range(1, planes):
            total = total + bufs[2][j].astype(jnp.float32)
        bufs[3][p0] = total.astype(jnp.bfloat16)
        for j in range(1, devs):
            spread_copy(bufs, j).start()

    def finish(bufs, down_out, up_out, up_pieces):
        for j in range(1, devs):
            spread_copy(bufs, j).wait_recv()
        width = down_out.shape[1] // devs
        up_width = 2 * up_out.shape[2] // up_pieces
        for p in range(devs):
            down_out[:, p * width : (p + 1) * width] = adapter_scale * bufs[3][
                p, :, :width
            ].astype(jnp.float32)
            if p < up_pieces:
                h, at = p // (up_pieces // 2), p % (up_pieces // 2)
                up_out[:, h, at * up_width : (at + 1) * up_width] = adapter_scale * bufs[3][
                    p, :, width:
                ].astype(jnp.float32)
        for j in range(1, devs):
            scatter_copy(bufs, j).wait_send()
            spread_copy(bufs, j).wait_send()
        for j in range(1, planes):
            plane_copy(bufs, j).wait_send()

    def project_down(bufs, act):
        width = x_ref.shape[1] // devs
        for p in range(devs):
            bufs[0][p, :, :width] = jnp.dot(
                act, x_ref[:, p * width : (p + 1) * width], preferred_element_type=jnp.float32
            ).astype(jnp.bfloat16)

    if with_adapters:
        for source, act in ((q_down_ref, q_down), (v_down_ref, v_down)):
            act[...] = lax.dot_general(
                source[...],
                x_ref[...],
                (((1,), (1,)), ((), ())),
                preferred_element_type=jnp.float32,
            ).astype(jnp.bfloat16)
        for h in range(2):
            q_up[h] = q_up_ref[:, h, :]
            v_up[h] = v_up_ref[:, h, :]
        q_act[...] = jnp.zeros_like(q_act)
        rank = q_act.shape[0]
        for p in range(2 * kv_heads, devs):
            v_bufs[0][p, :, x_ref.shape[1] // devs :] = jnp.zeros((rank, HEAD_SIZE), jnp.bfloat16)

    def stacked(ref, h, g):
        return jnp.concatenate(
            [
                ref[h, :, g * group_width + r * HEAD_SIZE : g * group_width + (r + 1) * HEAD_SIZE]
                for r in range(repeat)
            ],
            axis=0,
        )

    def send_parts(which, total, h, g, slots, limit):
        for d in range(slots):
            block = jnp.transpose(total[:, d * tok : (d + 1) * tok])
            if d == 0:
                own_part[which, h, g] = block
            else:
                part_send[which, h, g, d] = block.astype(jnp.bfloat16)
        for d in range(1, slots):

            @pl.when(d < limit)
            def _():
                return_copy(which, h, g, d).start()

    def probabilities(h, g, slots, limit):
        keys = slots * tok
        k = kv_buf[h, :slots, g, :, :HEAD_SIZE].reshape(keys, HEAD_SIZE)

        def one_head(r, inner):
            lanes = pl.ds(pl.multiple_of(g * group_width + r * HEAD_SIZE, HEAD_SIZE), HEAD_SIZE)
            at = pl.ds(pl.multiple_of(r * tok, tok), tok)
            s = lax.dot_general(
                q_ref[h, :, lanes],
                k,
                (((1,), (1,)), ((), ())),
                preferred_element_type=jnp.float32,
            )
            t = s * exponent + bias[int(slots == devs), :, :keys]
            e = jnp.exp2(t - jnp.max(t, axis=1, keepdims=True))
            w = e * (1.0 / jnp.sum(e, axis=1, keepdims=True))
            w_scr[g, at, :keys] = w
            p_scr[at, :keys] = w.astype(jnp.bfloat16)
            return inner

        lax.fori_loop(0, repeat, one_head, 0, unroll=2)
        dv = lax.dot_general(
            stacked(do_ref, h, g),
            p_scr[:, :keys],
            (((0,), (0,)), ((), ())),
            preferred_element_type=jnp.float32,
        )
        send_parts(1, dv, h, g, slots, limit)

    def score_gradients(h, g, slots, limit):
        keys = slots * tok
        k = kv_buf[h, :slots, g, :, :HEAD_SIZE].reshape(keys, HEAD_SIZE)
        v = kv_buf[h, :slots, g, :, HEAD_SIZE:].reshape(keys, HEAD_SIZE)

        def one_head(r, inner):
            lanes = pl.ds(pl.multiple_of(g * group_width + r * HEAD_SIZE, HEAD_SIZE), HEAD_SIZE)
            at = pl.ds(pl.multiple_of(r * tok, tok), tok)
            dp = lax.dot_general(
                do_ref[h, :, lanes],
                v,
                (((1,), (1,)), ((), ())),
                preferred_element_type=jnp.float32,
            )
            w = w_scr[g, at, :keys]
            low = w.astype(jnp.bfloat16).astype(jnp.float32)
            dot = jnp.sum(low * dp, axis=1, keepdims=True)
            ds = (w * (dp - dot)).astype(jnp.bfloat16)
            p_scr[at, :keys] = ds
            dq = jnp.dot(ds, k, preferred_element_type=jnp.float32) * scaling
            dq_ref[h, :, lanes] = dq.astype(jnp.bfloat16)
            return inner

        lax.fori_loop(0, repeat, one_head, 0, unroll=2)
        if with_adapters:
            lanes = slice(g * group_width, (g + 1) * group_width)
            dq_all = dq_ref[h, :, lanes]
            q_act[...] += lax.dot_general(
                q_up[h, :, lanes],
                dq_all,
                (((1,), (1,)), ((), ())),
                preferred_element_type=jnp.float32,
            )
            up = jnp.dot(q_down[...], dq_all, preferred_element_type=jnp.float32)
            up = up.astype(jnp.bfloat16)
            width = x_ref.shape[1] // devs
            each = group_width * 2 * kv_heads // devs
            pieces = group_width // each
            for i in range(pieces):
                q_bufs[0][(h * kv_heads + g) * pieces + i, :, width:] = up[
                    :, i * each : (i + 1) * each
                ]
        dk = lax.dot_general(
            stacked(q_ref, h, g),
            p_scr[:, :keys],
            (((0,), (0,)), ((), ())),
            preferred_element_type=jnp.float32,
        )
        send_parts(0, dk * scaling, h, g, slots, limit)

    def collect(which, out_ref):
        for d in range(1, devs):
            for g in range(kv_heads):

                @pl.when(ps + d < devs)
                def _():
                    return_copy(which, small, g, d).wait_recv()
                    own_part[which, small, g] += part_recv[which, small, g, d].astype(jnp.float32)

        for d in range(1, mid):
            for g in range(kv_heads):

                @pl.when(ps + d < mid)
                def _():
                    return_copy(which, big, g, d).wait_recv()
                    own_part[which, big, g] += part_recv[which, big, g, d].astype(jnp.float32)

        for h in range(2):
            for g in range(kv_heads):
                out_ref[h, :, g * HEAD_SIZE : (g + 1) * HEAD_SIZE] = own_part[which, h, g].astype(
                    jnp.bfloat16
                )

    def value_adapter():
        v_act = jnp.zeros(q_act.shape, jnp.float32)
        for h in range(2):
            v_act = v_act + lax.dot_general(
                v_up[h], gv_ref[h], (((1,), (1,)), ((), ())), preferred_element_type=jnp.float32
            )
            up = jnp.dot(v_down[...], gv_ref[h], preferred_element_type=jnp.float32)
            for g in range(kv_heads):
                v_bufs[0][h * kv_heads + g, :, x_ref.shape[1] // devs :] = up[
                    :, g * HEAD_SIZE : (g + 1) * HEAD_SIZE
                ].astype(jnp.bfloat16)
        project_down(v_bufs, v_act.astype(jnp.bfloat16))
        start_scatter(v_bufs)

    for d in range(1, mid):

        @pl.when(d <= ps)
        def _():
            gather_copy(small, d).wait_recv()

    for g in range(kv_heads):
        probabilities(small, g, mid, ps + 1)
    for g in range(kv_heads):
        score_gradients(small, g, mid, ps + 1)

    for d in range(1, devs):

        @pl.when(d <= ps + mid)
        def _():
            gather_copy(big, d).wait_recv()

    for g in range(kv_heads):
        probabilities(big, g, devs, ps + mid + 1)
    for g in range(kv_heads):
        score_gradients(big, g, devs, ps + mid + 1)
        if g == 0:
            collect(1, gv_ref)
            if with_adapters:
                value_adapter()

    if with_adapters:
        start_planes(v_bufs)
        project_down(q_bufs, q_act[...].astype(jnp.bfloat16))
        start_scatter(q_bufs)
        start_spread(v_bufs)
    collect(0, gk_ref)
    if with_adapters:
        start_planes(q_bufs)
        finish(v_bufs, vd_out, vu_out, 2 * kv_heads)
        start_spread(q_bufs)
        finish(q_bufs, qd_out, qu_out, devs)

    for d in range(1, devs):

        @pl.when(ps + d < devs)
        def _():
            gather_copy(small, d).wait_send()

        @pl.when(d <= ps + mid)
        def _():
            for which in range(2):
                for g in range(kv_heads):
                    return_copy(which, big, g, d).wait_send()

    for d in range(1, mid):

        @pl.when(ps + d < mid)
        def _():
            gather_copy(big, d).wait_send()

        @pl.when(d <= ps)
        def _():
            for which in range(2):
                for g in range(kv_heads):
                    return_copy(which, small, g, d).wait_send()


def attention_backward(q, do, k, v, seg, devs, adapters=None):
    tok, width = q.shape[1], q.shape[2]
    kv_heads = k.shape[2] // HEAD_SIZE
    repeat = width // k.shape[2]
    ctx = lax.axis_size("ctx")
    planes = ctx // devs
    bf16, f32 = jnp.bfloat16, jnp.float32
    vmem = pl.BlockSpec(memory_space=pltpu.VMEM)
    operands = (q, do, k, v, seg)
    results = [jax.ShapeDtypeStruct(a.shape, bf16) for a in (q, k, v)]
    scratch = [
        pltpu.VMEM((2, devs, kv_heads, tok, 2 * HEAD_SIZE), bf16),
        pltpu.VMEM((2, 2, kv_heads, devs, tok, HEAD_SIZE), bf16),
        pltpu.VMEM((2, 2, kv_heads, devs, tok, HEAD_SIZE), bf16),
        pltpu.VMEM((2, 2, kv_heads, tok, HEAD_SIZE), f32),
        pltpu.VMEM((repeat * tok, devs * tok), bf16),
        pltpu.VMEM((kv_heads, repeat * tok, devs * tok), f32),
        pltpu.VMEM((2, tok, devs * tok), f32),
        pltpu.SemaphoreType.DMA((2, devs)),
        pltpu.SemaphoreType.DMA((2, devs)),
        pltpu.SemaphoreType.DMA((2, 2, kv_heads, devs)),
        pltpu.SemaphoreType.DMA((2, 2, kv_heads, devs)),
    ]
    if adapters is not None:
        operands = operands + adapters
        x, q_down, v_down, q_up, v_up = adapters
        rank = q_down.shape[0]
        results += [jax.ShapeDtypeStruct(a.shape, f32) for a in (q_down, q_up, v_down, v_up)]
        scratch += [
            pltpu.VMEM((rank, tok), bf16),
            pltpu.VMEM((rank, tok), bf16),
            pltpu.VMEM((2, rank, q.shape[2]), bf16),
            pltpu.VMEM((2, rank, k.shape[2]), bf16),
            pltpu.VMEM((rank, tok), f32),
        ]
        for columns in ((x.shape[1] + 2 * width) // devs, x.shape[1] // devs + HEAD_SIZE):
            scratch += [
                pltpu.VMEM((n, rank, columns), bf16) for n in (devs, devs, planes, devs)
            ]
            scratch += [
                pltpu.SemaphoreType.DMA((n,)) for n in (devs, devs, planes, planes, devs, devs)
            ]
    return pl.pallas_call(
        functools.partial(attention_kernel, ctx, devs, adapters is not None),
        out_shape=tuple(results),
        in_specs=[vmem] * len(operands),
        out_specs=(vmem,) * len(results),
        scratch_shapes=scratch,
        compiler_params=pltpu.CompilerParams(
            collective_id=0, has_side_effects=True, vmem_limit_bytes=52 * 1024 * 1024
        ),
        name="attention_backward",
    )(*operands)


def on_device(
    projected_queries,
    projected_keys,
    projected_values,
    output_gradient,
    normed_layer_input,
    segment,
    query_adapter_down,
    query_adapter_up,
    value_adapter_down,
    value_adapter_up,
):
    tok_rows = projected_queries.shape[0]
    query_width = projected_queries.shape[2]
    key_width = projected_keys.shape[2]
    key_value_heads = key_width // HEAD_SIZE
    group_devs = GROUP // tok_rows
    whole_width = lax.axis_size("fsdp") == 1 and 2 * key_value_heads <= group_devs
    adapters = None
    if whole_width:
        adapters = (
            normed_layer_input,
            query_adapter_down,
            value_adapter_down,
            query_adapter_up,
            value_adapter_up,
        )
    query_grad, key_grad, value_grad, *totals = attention_backward(
        projected_queries.transpose(1, 0, 2),
        output_gradient.transpose(1, 0, 2),
        projected_keys.transpose(1, 0, 2),
        projected_values.transpose(1, 0, 2),
        segment.reshape(-1, tok_rows),
        group_devs,
        adapters,
    )
    grad_query = query_grad.transpose(1, 0, 2)
    grad_key = key_grad.transpose(1, 0, 2)
    grad_value = value_grad.transpose(1, 0, 2)
    if whole_width:
        return (grad_query, grad_key, grad_value, *totals)
    adapter_input = lax.psum(
        (
            jnp.dot(normed_layer_input, query_adapter_down.T, preferred_element_type=jnp.float32),
            jnp.dot(normed_layer_input, value_adapter_down.T, preferred_element_type=jnp.float32),
        ),
        "fsdp",
    )
    query_down_part = adapter_input[0].astype(jnp.bfloat16)
    value_down_part = adapter_input[1].astype(jnp.bfloat16)
    query_flattened_rows = grad_query.reshape(tok_rows, -1)
    value_flattened_rows = grad_value.reshape(tok_rows, -1)
    adapter_rank_rows = query_adapter_up.shape[0]
    adapter_output = lax.psum(
        (
            jnp.dot(
                query_flattened_rows,
                query_adapter_up.reshape(adapter_rank_rows, -1).T,
                preferred_element_type=jnp.float32,
            ),
            jnp.dot(
                value_flattened_rows,
                value_adapter_up.reshape(adapter_rank_rows, -1).T,
                preferred_element_type=jnp.float32,
            ),
        ),
        "fsdp",
    )
    query_up_part = adapter_output[0].astype(jnp.bfloat16)
    value_up_part = adapter_output[1].astype(jnp.bfloat16)
    local_down_query = jnp.dot(
        query_up_part.T, normed_layer_input, preferred_element_type=jnp.float32
    )
    local_up_query = jnp.dot(
        query_down_part.T, query_flattened_rows, preferred_element_type=jnp.float32
    ).reshape(adapter_rank_rows, 2, -1)
    local_down_value = jnp.dot(
        value_up_part.T, normed_layer_input, preferred_element_type=jnp.float32
    )
    local_up_value = jnp.dot(
        value_down_part.T, value_flattened_rows, preferred_element_type=jnp.float32
    ).reshape(adapter_rank_rows, 2, -1)
    gradient_totals = lax.psum(
        (local_down_query, local_up_query, local_down_value, local_up_value), "ctx"
    )
    return (
        grad_query,
        grad_key,
        grad_value,
        adapter_scale * gradient_totals[0],
        adapter_scale * gradient_totals[1],
        adapter_scale * gradient_totals[2],
        adapter_scale * gradient_totals[3],
    )


def solution(mesh):
    in_specs = (
        P(("rep", "ctx"), None, "fsdp"),
        P(("rep", "ctx"), None, "fsdp"),
        P(("rep", "ctx"), None, "fsdp"),
        P(("rep", "ctx"), None, "fsdp"),
        P(("rep", "ctx"), "fsdp"),
        P("rep"),
        P(None, "fsdp"),
        P(None, None, "fsdp"),
        P(None, "fsdp"),
        P(None, None, "fsdp"),
    )
    out_specs = (
        P(("rep", "ctx"), None, "fsdp"),
        P(("rep", "ctx"), None, "fsdp"),
        P(("rep", "ctx"), None, "fsdp"),
        P("rep", "fsdp"),
        P("rep", None, "fsdp"),
        P("rep", "fsdp"),
        P("rep", None, "fsdp"),
    )
    return jax.shard_map(
        on_device, mesh=mesh, in_specs=in_specs, out_specs=out_specs, check_vma=False
    )
```

time: 88.1 us -> 82.2 us (0.933)
  local copies, waits for them, and re-layouts: 17.6 us -> 12.6 us
    reshape x10 -> x0, local copies, waits for them, and re-layouts: 6.35 us -> none  [the longest x4 2.9 us: by_head(): return x.reshape(tok_rows, 2, heads, HEAD_SIZE).transpose(1, 2, 0, 3)]
    transpose x4 -> x2, local copies, waits for them, and re-layouts: 1.92 us -> 4.78 us  [the longest x1 3.79 us: on_device(): output_gradient.transpose(1, 0, 2)]
    unnamed x19, local copies, waits for them, and re-layouts: 9.34 us -> 7.85 us
where the time goes in v3:
time: 82.2 us; the launch traced here: 82 us
  Pallas kernels  68.7 us (84%)
  local copies, waits for them, and re-layouts  12.6 us (15%)
    pallas_call x1, Pallas kernels, attention_backward(): pl.pallas_call(functools.partial(attention_kernel, ctx, devs, adapters is...  68.7 us
    unnamed x19, local copies, waits for them, and re-layouts  7.85 us
    transpose x1, local copies, waits for them, and re-layouts, on_device(): output_gradient.transpose(1, 0, 2)  3.79 us

profile of v3, /device:TPU:0, one launch (start us, length us, event | category | flops | bytes accessed | tf_op | source)
XLA Modules:
  0.0 82.0 jit_solution(8529833204665095222)
XLA Ops:
  0.6 1.0 %copy_bitcast_fusion.2 = (bf16[2,128,256]{2,1,0:T(8,128)(2,1)S(1)}, bf16[2,128,256]{2,1,0:T(8,128)(2,1)S(1)}) fusion(bf16[128,2,256]{2,1,0:T(2,128)(2,1)} %param.12, bf16[128,2,256]{2,1,0:T(2,128)(2,1)} %param.11), kind=kLoop, calls=%fused_computation.2 | loop fusion | bytes 524288 | tf_op jit(solution)/shard_map/transpose | solution.py:539
  1.6 0.0 copy-start
  1.6 0.0 copy-start.1
  1.7 0.0 copy-start.2
  1.7 0.0 copy-start.3
  1.7 0.0 copy-start.4
  1.7 3.8 %copy_bitcast_fusion = (bf16[2,128,2048]{2,1,0:T(8,128)(2,1)}, bf16[2,128,2048]{2,1,0:T(8,128)(2,1)}) fusion(bf16[128,2,2048]{2,1,0:T(2,128)(2,1)} %param.13, bf16[128,2,2048]{2,1,0:T(2,128)(2,1)} %param.10), kind=kLoop, calls=%fused_computation | loop fusion | bytes 4194304 | tf_op jit(solution)/shard_map/transpose | solution.py:537
  5.5 0.0 copy-done
  5.5 0.0 copy-done.1
  5.5 0.0 copy-done.2
  5.5 0.0 copy-done.3
  5.5 0.0 copy-done.4
  5.5 68.7 %attention_backward.1 = (bf16[2,128,2048]{2,1,0:T(8,128)(2,1)}, bf16[2,128,256]{2,1,0:T(8,128)(2,1)S(1)}, bf16[2,128,256]{2,1,0:T(8,128)(2,1)S(1)}, f32[16,8192]...) custom-call(bf16[2,128,2048]{2,1,0:T(8,128)(2,1)} %get-tuple-element.29.q_ref, ...), custom_call_target="tpu_custom_call" | custom-call | tf_op jit(solution)/shard_map/attention_backward/pallas_call | solution.py:495
  74.2 0.0 copy-start.5
  74.2 3.3 %copy.21 = bf16[128,2,2048]{2,1,0:T(2,128)(2,1)} copy(bf16[128,2,2048]{2,0,1:T(8,128)(2,1)} %bitcast.15) | data formatting | bytes 2097152
  77.5 0.8 copy.22
  78.3 0.8 copy.23
  79.1 0.8 copy.32
  79.9 0.7 copy.33
  80.6 0.0 copy-done.5
  80.6 0.8 copy.34
  81.4 0.6 copy.35
Async XLA Ops:
  1.6 3.9 %copy-start = (bf16[16,8192]{1,0:T(8,128)(2,1)S(1)}, bf16[16,8192]{1,0:T(8,128)(2,1)}, u32[]{:S(2)}) copy-start(bf16[16,8192]{1,0:T(8,128)(2,1)} %refs_1_.1) | copy-start | bytes 786436
  1.6 3.8 %copy-start.1 = (bf16[16,8192]{1,0:T(8,128)(2,1)S(1)}, bf16[16,8192]{1,0:T(8,128)(2,1)}, u32[]{:S(2)}) copy-start(bf16[16,8192]{1,0:T(8,128)(2,1)} %refs_2_.1) | copy-start | bytes 786436
  1.7 3.8 %copy-start.2 = (bf16[16,2,2048]{2,1,0:T(2,128)(2,1)S(1)}, bf16[16,2,2048]{2,1,0:T(2,128)(2,1)}, u32[]{:S(2)}) copy-start(bf16[16,2,2048]{2,1,0:T(2,128)(2,1)} %refs_3_.1) | copy-start | bytes 393220
  1.7 3.8 %copy-start.3 = (s32[4096]{0:T(1024)S(1)}, s32[4096]{0:T(1024)}, u32[]{:S(2)}) copy-start(s32[4096]{0:T(1024)} %param.15) | copy-start | bytes 49156
  1.7 3.8 %copy-start.4 = (bf16[16,2,256]{2,1,0:T(2,128)(2,1)S(1)}, bf16[16,2,256]{2,1,0:T(2,128)(2,1)}, u32[]{:S(2)}) copy-start(bf16[16,2,256]{2,1,0:T(2,128)(2,1)} %refs_4_.1) | copy-start | bytes 49156
  74.2 6.4 %copy-start.5 = (f32[16,8192]{1,0:T(8,128)S(1)}, f32[16,8192]{1,0:T(8,128)}, u32[]{:S(2)}) copy-start(f32[16,8192]{1,0:T(8,128)} %get-tuple-element.44) | copy-start | bytes 1572868

commit v4 on v3

--- a/solution.py
+++ b/solution.py
@@ -291,7 +291,7 @@
             p_scr[at, :keys] = w.astype(jnp.bfloat16)
             return inner
 
-        lax.fori_loop(0, repeat, one_head, 0, unroll=2)
+        lax.fori_loop(0, repeat, one_head, 0, unroll=8)
         dv = lax.dot_general(
             stacked(do_ref, h, g),
             p_scr[:, :keys],
@@ -323,7 +323,7 @@
             dq_ref[h, :, lanes] = dq.astype(jnp.bfloat16)
             return inner
 
-        lax.fori_loop(0, repeat, one_head, 0, unroll=2)
+        lax.fori_loop(0, repeat, one_head, 0, unroll=8)
         if with_adapters:
             lanes = slice(g * group_width, (g + 1) * group_width)
             dq_all = dq_ref[h, :, lanes]
@@ -414,15 +414,15 @@
                 value_adapter()
 
     if with_adapters:
-        start_planes(v_bufs)
         project_down(q_bufs, q_act[...].astype(jnp.bfloat16))
         start_scatter(q_bufs)
+        start_planes(v_bufs)
+        start_planes(q_bufs)
         start_spread(v_bufs)
+        start_spread(q_bufs)
     collect(0, gk_ref)
     if with_adapters:
-        start_planes(q_bufs)
         finish(v_bufs, vd_out, vu_out, 2 * kv_heads)
-        start_spread(q_bufs)
         finish(q_bufs, qd_out, qu_out, devs)
 
     for d in range(1, devs):

time: 82.2 us -> 80.5 us (0.979)
  Pallas kernels: 68.7 us -> 67 us
    pallas_call x1, Pallas kernels: 68.7 us -> 67 us  [attention_backward(): pl.pallas_call(functools.partial(attention_kernel, ctx, devs, adapters is...]
where the time goes in v4:
time: 80.5 us; the launch traced here: 80.3 us
  Pallas kernels  67 us (83%)
  local copies, waits for them, and re-layouts  12.6 us (16%)
    pallas_call x1, Pallas kernels, attention_backward(): pl.pallas_call(functools.partial(attention_kernel, ctx, devs, adapters is...  67 us
    unnamed x19, local copies, waits for them, and re-layouts  7.85 us
    transpose x1, local copies, waits for them, and re-layouts, on_device(): output_gradient.transpose(1, 0, 2)  3.79 us

profile of v4, /device:TPU:0, one launch (start us, length us, event | category | flops | bytes accessed | tf_op | source)
XLA Modules:
  0.0 80.3 jit_solution(2331170507203566835)
XLA Ops:
  0.6 1.0 %copy_bitcast_fusion.2 = (bf16[2,128,256]{2,1,0:T(8,128)(2,1)S(1)}, bf16[2,128,256]{2,1,0:T(8,128)(2,1)S(1)}) fusion(bf16[128,2,256]{2,1,0:T(2,128)(2,1)} %param.12, bf16[128,2,256]{2,1,0:T(2,128)(2,1)} %param.11), kind=kLoop, calls=%fused_computation.2 | loop fusion | bytes 524288 | tf_op jit(solution)/shard_map/transpose | solution.py:539
  1.6 0.0 copy-start
  1.6 0.0 copy-start.1
  1.7 0.0 copy-start.2
  1.7 0.0 copy-start.3
  1.7 0.0 copy-start.4
  1.7 3.8 %copy_bitcast_fusion = (bf16[2,128,2048]{2,1,0:T(8,128)(2,1)}, bf16[2,128,2048]{2,1,0:T(8,128)(2,1)}) fusion(bf16[128,2,2048]{2,1,0:T(2,128)(2,1)} %param.13, bf16[128,2,2048]{2,1,0:T(2,128)(2,1)} %param.10), kind=kLoop, calls=%fused_computation | loop fusion | bytes 4194304 | tf_op jit(solution)/shard_map/transpose | solution.py:537
  5.5 0.0 copy-done
  5.5 0.0 copy-done.1
  5.5 0.0 copy-done.2
  5.5 0.0 copy-done.3
  5.5 0.0 copy-done.4
  5.5 67.0 %attention_backward.1 = (bf16[2,128,2048]{2,1,0:T(8,128)(2,1)}, bf16[2,128,256]{2,1,0:T(8,128)(2,1)S(1)}, bf16[2,128,256]{2,1,0:T(8,128)(2,1)S(1)}, f32[16,8192]...) custom-call(bf16[2,128,2048]{2,1,0:T(8,128)(2,1)} %get-tuple-element.29.q_ref, ...), custom_call_target="tpu_custom_call" | custom-call | tf_op jit(solution)/shard_map/attention_backward/pallas_call | solution.py:495
  72.5 0.0 copy-start.5
  72.5 3.3 %copy.21 = bf16[128,2,2048]{2,1,0:T(2,128)(2,1)} copy(bf16[128,2,2048]{2,0,1:T(8,128)(2,1)} %bitcast.15) | data formatting | bytes 2097152
  75.8 0.8 copy.22
  76.6 0.8 copy.23
  77.4 0.8 copy.32
  78.2 0.7 copy.33
  78.9 0.0 copy-done.5
  78.9 0.8 copy.34
  79.7 0.6 copy.35
Async XLA Ops:
  1.6 3.9 %copy-start = (bf16[16,8192]{1,0:T(8,128)(2,1)S(1)}, bf16[16,8192]{1,0:T(8,128)(2,1)}, u32[]{:S(2)}) copy-start(bf16[16,8192]{1,0:T(8,128)(2,1)} %refs_1_.1) | copy-start | bytes 786436
  1.6 3.8 %copy-start.1 = (bf16[16,8192]{1,0:T(8,128)(2,1)S(1)}, bf16[16,8192]{1,0:T(8,128)(2,1)}, u32[]{:S(2)}) copy-start(bf16[16,8192]{1,0:T(8,128)(2,1)} %refs_2_.1) | copy-start | bytes 786436
  1.7 3.8 %copy-start.2 = (bf16[16,2,2048]{2,1,0:T(2,128)(2,1)S(1)}, bf16[16,2,2048]{2,1,0:T(2,128)(2,1)}, u32[]{:S(2)}) copy-start(bf16[16,2,2048]{2,1,0:T(2,128)(2,1)} %refs_3_.1) | copy-start | bytes 393220
  1.7 3.8 %copy-start.3 = (s32[4096]{0:T(1024)S(1)}, s32[4096]{0:T(1024)}, u32[]{:S(2)}) copy-start(s32[4096]{0:T(1024)} %param.15) | copy-start | bytes 49156
  1.7 3.8 %copy-start.4 = (bf16[16,2,256]{2,1,0:T(2,128)(2,1)S(1)}, bf16[16,2,256]{2,1,0:T(2,128)(2,1)}, u32[]{:S(2)}) copy-start(bf16[16,2,256]{2,1,0:T(2,128)(2,1)} %refs_4_.1) | copy-start | bytes 49156
  72.5 6.4 %copy-start.5 = (f32[16,8192]{1,0:T(8,128)S(1)}, f32[16,8192]{1,0:T(8,128)}, u32[]{:S(2)}) copy-start(f32[16,8192]{1,0:T(8,128)} %get-tuple-element.44) | copy-start | bytes 1572868
